TPU v7x, 32 devices: a whole 2x2x4 slice. The times are simulated.
32 devices in a mesh: dp: 8 (over z, core), tensor: 4 (over y, x).
Axes of the slice: x: 2, y: 2, z: 4, core: 2. Of those that a mesh axis runs over, the one named last changes fastest.
Arguments:
- tokens: bfloat16 [12288, 2048], P(('dp', 'tensor')), may hold values from -6 to 6
- cotangent: bfloat16 [12288, 2048], P(('dp', 'tensor')), may hold values from -6 to 6
- prompt_len: int32 [4], replicated, may hold values from 512 to 1024, as said below
- cont_len: int32 [4, 8], P(None, 'dp'), may hold values from 1 to 256, as said below
- w_query: bfloat16 [2048, 2048], P('dp', 'tensor'), may hold values from -0.5 to 0.5
- key_weight: bfloat16 [2048, 512], P('dp', 'tensor'), may hold values from -0.5 to 0.5
- value_weight: bfloat16 [2048, 512], P('dp', 'tensor'), may hold values from -0.125 to 0.125
- w_out: bfloat16 [2048, 2048], P('tensor', 'dp'), may hold values from -2 to 2
- w_gate: bfloat16 [2048, 8192], P('dp', 'tensor'), may hold values from -0.125 to 0.125
- w_up: bfloat16 [2048, 8192], P('dp', 'tensor'), may hold values from -0.125 to 0.125
- w_down: bfloat16 [8192, 2048], P('tensor', 'dp'), may hold values from -0.5 to 0.5
- attn_gain: bfloat16 [2048], P('dp'), may hold values from 0.5 to 1.5
- ffn_gain: bfloat16 [2048], P('dp'), may hold values from 0.5 to 1.5
Outputs:
- output: bfloat16 [12288, 2048], P(('dp', 'tensor'))
- input_grad: float32 [12288, 2048], P(('dp', 'tensor'))
- grad_query: float32 [2048, 2048], P('dp', 'tensor')
- grad_key: float32 [2048, 512], P('dp', 'tensor')
- grad_value: float32 [2048, 512], P('dp', 'tensor')
- grad_out: float32 [2048, 2048], P('tensor', 'dp')
- grad_gate: float32 [2048, 8192], P('dp', 'tensor')
- grad_up: float32 [2048, 8192], P('dp', 'tensor')
- grad_down: float32 [8192, 2048], P('tensor', 'dp')
- grad_attn_gain: float32 [2048], P(('dp', 'tensor'))
- grad_ffn_gain: float32 [2048], P(('dp', 'tensor'))
Inputs may be any that keep to these rules, and one draw needn't show every extreme that they name: `prompt_len`: prompt slots of a group beyond its length are padding; some group has exactly 1024 prompt tokens. `cont_len`: slots of a continuation beyond its length are padding; in each group some continuation has exactly 256 tokens.
All inputs are finite; a program needn't handle non-finite values.
Results may differ from a plain program's by a relative error of at most 0.024.
Values may be sent and summed in bfloat16 or wider, within the bound.
No kernel may reach another device: no remote copies, remote signals or barrier semaphores. Data moves between devices by JAX's collectives and lax.ppermute only.
A program may use at most 256 MiB of HBM per device.

v0:
```python
import jax
import jax.numpy as jnp
from jax import lax
from jax.sharding import PartitionSpec as P

HEAD_SIZE = 64
NG = 4
PROMPT_DEV = 128
CONT = 256


EPS = 1e-05
THETA = 10000000.0
ATTN_SCALE = 0.015625
RESID_SCALE = 0.22
NEG_FILL = -1e30


def project(left_mat, right_mat):
    return jnp.dot(left_mat, right_mat, preferred_element_type=jnp.float32)


def dot_rows(left_mat, right_mat):
    return lax.dot_general(
        left_mat, right_mat, (((0,), (0,)), ((), ())), preferred_element_type=jnp.float32
    )


def dot_back(left_mat, right_mat):
    return lax.dot_general(
        left_mat, right_mat, (((1,), (1,)), ((), ())), preferred_element_type=jnp.float32
    )


def rope_tables(positions, head_width):
    half_width = head_width // 2
    frequency = THETA ** (-(jnp.arange(half_width).astype(jnp.float32) * 2.0) / head_width)
    angles = positions.astype(jnp.float32)[:, None] * frequency[None, :]
    angles = jnp.concatenate([angles, angles], axis=1)
    return (jnp.cos(angles), jnp.sin(angles))


def apply_rotary(values, cosine_table, sine_values):
    half_width = values.shape[-1] // 2
    turned = jnp.concatenate([-values[..., half_width:], values[..., :half_width]], axis=-1)
    return values * cosine_table[:, None, :] + turned * sine_values[:, None, :]


def unrotate(values, cosine_table, sine_values):
    half_width = values.shape[-1] // 2
    scaled_sin = values * sine_values[:, None, :]
    turned = jnp.concatenate([scaled_sin[..., half_width:], -scaled_sin[..., :half_width]], axis=-1)
    return values * cosine_table[:, None, :] + turned


def build_mask(base_row, prompt_length, portion_rows, cont_rows, prompt_row_count):
    row_ids = jnp.arange(portion_rows + cont_rows)[:, None]
    key_ids = jnp.arange(prompt_row_count + cont_rows)[None, :]
    in_prompt = key_ids < prompt_row_count
    prompt_part = in_prompt & (key_ids <= base_row + row_ids)
    cont_part = jnp.where(
        in_prompt, key_ids < prompt_length, key_ids - prompt_row_count <= row_ids - portion_rows
    )
    return jnp.where(row_ids < portion_rows, prompt_part, cont_part)


def norm_parts(values):
    row_scale = lax.rsqrt(jnp.mean(values * values, axis=-1, keepdims=True) + EPS)
    return (values * row_scale, row_scale)


def norm_back(grad_norm, unit_rows, row_scale, gain_vec):
    scaled = grad_norm * gain_vec
    grad_in = row_scale * (
        scaled - unit_rows * jnp.mean(scaled * unit_rows, axis=-1, keepdims=True)
    )
    return (grad_in, jnp.sum(grad_norm * unit_rows, axis=0))


def gather_rows(local_rows):
    return lax.all_gather(local_rows, "tensor", axis=0, tiled=True)


def reduce_rows(row_terms):
    return lax.psum_scatter(row_terms, "tensor", scatter_dimension=0, tiled=True)


def score_block(single_query, every_key, key_mask):
    score_matrix = (
        jnp.einsum("wclz,icz->clwi", single_query, every_key, preferred_element_type=jnp.float32)
        * ATTN_SCALE
    )
    return jnp.where(key_mask[None, None], score_matrix, NEG_FILL)


def local(
    tokens,
    cotangent,
    prompt_len,
    cont_len,
    w_query,
    key_weight,
    value_weight,
    w_out,
    w_gate,
    w_up,
    w_down,
    attn_gain,
    ffn_gain,
):
    portion_rows = PROMPT_DEV
    block_row_set = PROMPT_DEV + CONT
    prompt_row_count = PROMPT_DEV * lax.axis_size("dp")
    dp_index = lax.axis_index("dp")
    local_rows = tokens.shape[0]
    row_start = lax.axis_index("tensor") * local_rows
    head_count = w_query.shape[1] // HEAD_SIZE
    group_count = key_weight.shape[1] // HEAD_SIZE
    repeat = head_count // group_count
    full_query, full_key, full_value, full_out, gain_one = (
        lax.all_gather(w_query, "dp", axis=0, tiled=True),
        lax.all_gather(key_weight, "dp", axis=0, tiled=True),
        lax.all_gather(value_weight, "dp", axis=0, tiled=True),
        lax.all_gather(w_out, "dp", axis=1, tiled=True),
        lax.all_gather(attn_gain, "dp", axis=0, tiled=True),
    )
    col_ids = jnp.arange(block_row_set)[None, :]
    starts = prompt_len[:, None]
    positions = jnp.where(
        col_ids < portion_rows, dp_index * portion_rows + col_ids, starts + col_ids - portion_rows
    ).reshape(-1)
    valid_rows = jnp.where(
        col_ids < portion_rows,
        dp_index * portion_rows + col_ids < starts,
        col_ids - portion_rows < cont_len,
    ).reshape(-1)
    valid_local = lax.dynamic_slice_in_dim(valid_rows.astype(jnp.float32), row_start, local_rows)
    cosine_table, sine_values = rope_tables(positions, HEAD_SIZE)
    resid_in = tokens.astype(jnp.float32)
    unit_one, scale_one = norm_parts(resid_in)
    normed = gather_rows((unit_one * gain_one).astype(jnp.bfloat16))
    query_proj = project(normed, full_query)
    key_projected = project(normed, full_key)
    value_rows = project(normed, full_value).astype(jnp.bfloat16)
    query_rot = apply_rotary(
        query_proj.reshape(-1, head_count, HEAD_SIZE), cosine_table, sine_values
    ).astype(jnp.bfloat16)
    key_rotated = apply_rotary(
        key_projected.reshape(-1, group_count, HEAD_SIZE), cosine_table, sine_values
    ).astype(jnp.bfloat16)
    query_grp = query_rot.reshape(NG, block_row_set, group_count, repeat, HEAD_SIZE)
    key_grp = key_rotated.reshape(NG, block_row_set, group_count, HEAD_SIZE)
    value_grp = value_rows.reshape(NG, block_row_set, group_count, HEAD_SIZE)
    prompt_key_rows, prompt_value_rows = (
        lax.all_gather(key_grp[:, :portion_rows], "dp", axis=1, tiled=True),
        lax.all_gather(value_grp[:, :portion_rows], "dp", axis=1, tiled=True),
    )

    def forward_group(group_items):
        single_query, key_one, value_one, key_prompt, value_prompt, length_one = group_items
        key_mask = build_mask(
            dp_index * portion_rows, length_one, portion_rows, CONT, prompt_row_count
        )
        every_key = jnp.concatenate([key_prompt, key_one[portion_rows:]], axis=0)
        every_value = jnp.concatenate([value_prompt, value_one[portion_rows:]], axis=0)
        score_matrix = score_block(single_query, every_key, key_mask)
        row_top = jnp.max(score_matrix, axis=-1, keepdims=True)
        weights = jnp.exp(score_matrix - row_top)
        row_total = jnp.sum(weights, axis=-1, keepdims=True)
        probability_rows = (weights / row_total).astype(jnp.bfloat16)
        mixed_one = jnp.einsum(
            "yxks,syt->kyxt", probability_rows, every_value, preferred_element_type=jnp.float32
        )
        return (mixed_one.reshape(block_row_set, head_count * HEAD_SIZE), row_top, row_total)

    merged_heads, row_tops, row_totals = lax.map(
        forward_group,
        (query_grp, key_grp, value_grp, prompt_key_rows, prompt_value_rows, prompt_len),
    )
    mixed_rows = merged_heads.reshape(NG * block_row_set, head_count * HEAD_SIZE).astype(
        jnp.bfloat16
    )
    attn_out = reduce_rows(project(mixed_rows, full_out))
    hidden = resid_in + RESID_SCALE * attn_out
    full_gate, full_up, full_down, gain_two = (
        lax.all_gather(w_gate, "dp", axis=0, tiled=True),
        lax.all_gather(w_up, "dp", axis=0, tiled=True),
        lax.all_gather(w_down, "dp", axis=1, tiled=True),
        lax.all_gather(ffn_gain, "dp", axis=0, tiled=True),
    )
    unit_two, scale_two = norm_parts(hidden)
    normed_two = gather_rows((unit_two * gain_two).astype(jnp.bfloat16))
    gate_val = project(normed_two, full_gate)
    up_val = project(normed_two, full_up)
    sigmoid_gate = jax.nn.sigmoid(gate_val)
    product = (gate_val * sigmoid_gate * up_val).astype(jnp.bfloat16)
    ffn_out = reduce_rows(project(product, full_down))
    output = (hidden + RESID_SCALE * ffn_out).astype(jnp.bfloat16)
    grad_y = cotangent.astype(jnp.float32) * valid_local[:, None]
    full_gate, full_up, full_down, gain_two = (
        lax.all_gather(w_gate, "dp", axis=0, tiled=True),
        lax.all_gather(w_up, "dp", axis=0, tiled=True),
        lax.all_gather(w_down, "dp", axis=1, tiled=True),
        lax.all_gather(ffn_gain, "dp", axis=0, tiled=True),
    )
    grad_ffn = gather_rows((RESID_SCALE * grad_y).astype(jnp.bfloat16))
    grad_prod = dot_back(grad_ffn, full_down)
    grad_down = dot_rows(product, grad_ffn)
    grad_gate_val = (
        grad_prod * up_val * sigmoid_gate * (1.0 + gate_val * (1.0 - sigmoid_gate))
    ).astype(jnp.bfloat16)
    grad_up_val = (grad_prod * gate_val * sigmoid_gate).astype(jnp.bfloat16)
    grad_gate_w = dot_rows(normed_two, grad_gate_val)
    grad_up_w = dot_rows(normed_two, grad_up_val)
    grad_normed_two = reduce_rows(
        dot_back(grad_gate_val, full_gate) + dot_back(grad_up_val, full_up)
    )
    grad_hidden_norm, gain_two_part = norm_back(grad_normed_two, unit_two, scale_two, gain_two)
    grad_hidden = grad_y + grad_hidden_norm
    ffn_grads = (
        lax.psum_scatter(
            grad_gate_w.astype(jnp.bfloat16), "dp", scatter_dimension=0, tiled=True
        ).astype(jnp.float32),
        lax.psum_scatter(
            grad_up_w.astype(jnp.bfloat16), "dp", scatter_dimension=0, tiled=True
        ).astype(jnp.float32),
        lax.psum_scatter(
            grad_down.astype(jnp.bfloat16), "dp", scatter_dimension=1, tiled=True
        ).astype(jnp.float32),
        lax.psum_scatter(
            gain_two_part.astype(jnp.bfloat16), "dp", scatter_dimension=0, tiled=True
        ).astype(jnp.float32),
    )
    full_query, full_key, full_value, full_out, gain_one = (
        lax.all_gather(w_query, "dp", axis=0, tiled=True),
        lax.all_gather(key_weight, "dp", axis=0, tiled=True),
        lax.all_gather(value_weight, "dp", axis=0, tiled=True),
        lax.all_gather(w_out, "dp", axis=1, tiled=True),
        lax.all_gather(attn_gain, "dp", axis=0, tiled=True),
    )
    grad_attn = gather_rows((RESID_SCALE * grad_hidden).astype(jnp.bfloat16))
    grad_mixed = dot_back(grad_attn, full_out).astype(jnp.bfloat16)
    grad_out_w = dot_rows(mixed_rows, grad_attn)
    grad_grp = grad_mixed.reshape(NG, block_row_set, group_count, repeat, HEAD_SIZE)

    def backward_group(group_items):
        (
            single_query,
            key_one,
            value_one,
            key_prompt,
            value_prompt,
            length_one,
            row_top,
            row_total,
            single_gradient,
        ) = group_items
        key_mask = build_mask(
            dp_index * portion_rows, length_one, portion_rows, CONT, prompt_row_count
        )
        every_key = jnp.concatenate([key_prompt, key_one[portion_rows:]], axis=0)
        every_value = jnp.concatenate([value_prompt, value_one[portion_rows:]], axis=0)
        score_matrix = score_block(single_query, every_key, key_mask)
        probability_rows = jnp.exp(score_matrix - row_top) / row_total
        grad_probs = jnp.einsum(
            "wclz,icz->clwi", single_gradient, every_value, preferred_element_type=jnp.float32
        )
        row_inner = jnp.sum(probability_rows * grad_probs, axis=-1, keepdims=True)
        score_gradient = (probability_rows * (grad_probs - row_inner)).astype(jnp.bfloat16)
        grad_query_one = (
            jnp.einsum(
                "yxks,syt->kyxt", score_gradient, every_key, preferred_element_type=jnp.float32
            )
            * ATTN_SCALE
        )
        grad_key_one = (
            jnp.einsum(
                "kjsv,skjb->vkb", score_gradient, single_query, preferred_element_type=jnp.float32
            )
            * ATTN_SCALE
        )
        grad_value_one = jnp.einsum(
            "kjsv,skjb->vkb",
            probability_rows.astype(jnp.bfloat16),
            single_gradient,
            preferred_element_type=jnp.float32,
        )
        return (
            grad_query_one.reshape(block_row_set, head_count * HEAD_SIZE),
            grad_key_one,
            grad_value_one,
        )

    grad_q_all, grad_k_all, grad_v_all = lax.map(
        backward_group,
        (
            query_grp,
            key_grp,
            value_grp,
            prompt_key_rows,
            prompt_value_rows,
            prompt_len,
            row_tops,
            row_totals,
            grad_grp,
        ),
    )
    prompt_key_grad, prompt_val_grad = (
        lax.psum_scatter(
            grad_k_all[:, :prompt_row_count].astype(jnp.bfloat16),
            "dp",
            scatter_dimension=1,
            tiled=True,
        ).astype(jnp.float32),
        lax.psum_scatter(
            grad_v_all[:, :prompt_row_count].astype(jnp.bfloat16),
            "dp",
            scatter_dimension=1,
            tiled=True,
        ).astype(jnp.float32),
    )
    key_grad_rot = jnp.concatenate(
        [prompt_key_grad, grad_k_all[:, prompt_row_count:]], axis=1
    ).reshape(-1, group_count, HEAD_SIZE)
    value_grad = (
        jnp.concatenate([prompt_val_grad, grad_v_all[:, prompt_row_count:]], axis=1)
        .reshape(-1, group_count * HEAD_SIZE)
        .astype(jnp.bfloat16)
    )
    query_grad = (
        unrotate(grad_q_all.reshape(-1, head_count, HEAD_SIZE), cosine_table, sine_values)
        .reshape(-1, head_count * HEAD_SIZE)
        .astype(jnp.bfloat16)
    )
    key_grad = (
        unrotate(key_grad_rot, cosine_table, sine_values)
        .reshape(-1, group_count * HEAD_SIZE)
        .astype(jnp.bfloat16)
    )
    grad_normed = reduce_rows(
        dot_back(query_grad, full_query)
        + dot_back(key_grad, full_key)
        + dot_back(value_grad, full_value)
    )
    grad_query_w = dot_rows(normed, query_grad)
    grad_key_w = dot_rows(normed, key_grad)
    grad_value_w = dot_rows(normed, value_grad)
    grad_input_norm, gain_one_part = norm_back(grad_normed, unit_one, scale_one, gain_one)
    input_grad = grad_hidden + grad_input_norm
    attn_grads = (
        lax.psum_scatter(
            grad_query_w.astype(jnp.bfloat16), "dp", scatter_dimension=0, tiled=True
        ).astype(jnp.float32),
        lax.psum_scatter(
            grad_key_w.astype(jnp.bfloat16), "dp", scatter_dimension=0, tiled=True
        ).astype(jnp.float32),
        lax.psum_scatter(
            grad_value_w.astype(jnp.bfloat16), "dp", scatter_dimension=0, tiled=True
        ).astype(jnp.float32),
        lax.psum_scatter(
            grad_out_w.astype(jnp.bfloat16), "dp", scatter_dimension=1, tiled=True
        ).astype(jnp.float32),
        lax.psum_scatter(
            gain_one_part.astype(jnp.bfloat16), "dp", scatter_dimension=0, tiled=True
        ).astype(jnp.float32),
    )
    gain_grads = (
        lax.psum_scatter(attn_grads[4], "tensor", scatter_dimension=0, tiled=True),
        lax.psum_scatter(ffn_grads[3], "tensor", scatter_dimension=0, tiled=True),
    )
    return (
        output,
        input_grad,
        attn_grads[0],
        attn_grads[1],
        attn_grads[2],
        attn_grads[3],
        ffn_grads[0],
        ffn_grads[1],
        ffn_grads[2],
        gain_grads[0],
        gain_grads[1],
    )


def solution(mesh):
    placed = (
        P(("dp", "tensor"), None),
        P(("dp", "tensor"), None),
        P(),
        P(None, "dp"),
        P("dp", "tensor"),
        P("dp", "tensor"),
        P("dp", "tensor"),
        P("tensor", "dp"),
        P("dp", "tensor"),
        P("dp", "tensor"),
        P("tensor", "dp"),
        P("dp"),
        P("dp"),
    )
    return jax.shard_map(
        local,
        mesh=mesh,
        in_specs=placed,
        out_specs=(
            P(("dp", "tensor"), None),
            P(("dp", "tensor"), None),
            P("dp", "tensor"),
            P("dp", "tensor"),
            P("dp", "tensor"),
            P("tensor", "dp"),
            P("dp", "tensor"),
            P("dp", "tensor"),
            P("tensor", "dp"),
            P(("dp", "tensor")),
            P(("dp", "tensor")),
        ),
        check_vma=False,
    )
```

profile of v0, /device:TPU:0, one launch (start us, length us, event | category | flops | bytes accessed | tf_op | source)
XLA Modules:
  0.0 2023.1 jit_solution(5303339663855243421)
XLA Ops:
  7.9 13.5 all-gather
  30.7 14.9 all_gather.58
  45.6 49.5 %all-gather.14.cloned.1.call-done = bf16[1536,2048]{1,0:T(8,128)(2,1)} async-done(((bf16[384,2048]{1,0:T(8,128)(2,1)}), bf16[1536,2048]{1,0:T(8,128)(2,1)}) %all-gather.14.cloned.1.call-update) | async-done | bytes 6291472 | tf_op jit(solution)/shard_map/all_gather | solution.py:81
  101.9 17.4 all_gather.56
  129.8 8.6 fusion.82
  156.3 23.1 %all-gather.16.cloned.1.call-done = bf16[4,1024,2,64]{1,0,3,2:T(4,128)(2,1)} async-done(((bf16[4,128,2,64]{1,0,3,2:T(4,128)(2,1)}), bf16[4,1024,2,64]{1,0,3,2:T(4,128)(2,1)}) %all-gather.16.cloned.1.call-update) | async-done | bytes 1048592 | tf_op jit(solution)/shard_map/all_gather | solution.py:156
  181.9 140.3 %while.32 = (s32[]{:T(128)}, bf16[4,384,512]{2,1,0:T(8,128)(2,1)}, f32[4,2,4,384,1]{3,2,1,4,0:T(4,128)}, f32[4,2,4,384,1]{3,2,1,4,0:T(4,128)}, bf16[4,1024,2,64]...) while((s32[]{:T(128)}, bf16[4,384,512]{2,1,0:T(8,128)(2,1)}, ...), condition=%wide.region_4.5_spmd, body=%wide.region_1.4_spmd.sunk | while | flops 1057586048 | bytes 54660560 | solution.py:176
  187.0 6.9 fusion.151
  193.9 8.9 fusion.152
  202.8 8.7 fusion.153
  219.6 6.9 fusion.151
  226.5 8.7 fusion.152
  235.2 8.6 fusion.153
  252.0 6.9 fusion.151
  258.9 8.7 fusion.152
  267.6 8.6 fusion.153
  284.4 6.9 fusion.151
  291.3 8.7 fusion.152
  300.0 8.6 fusion.153
  322.3 11.0 fusion.83
  334.2 10.7 all-gather.1
  344.9 108.0 %reduce-scatter.18.cloned.1.call-done = f32[384,2048]{1,0:T(8,128)} async-done(((f32[1536,2048]{1,0:T(8,128)}), f32[384,2048]{1,0:T(8,128)}) %reduce-scatter.18.cloned.1.call-update) | async-done | bytes 3145744 | tf_op jit(solution)/shard_map/reduce_scatter | solution.py:85
  462.6 74.0 %all-gather.26.cloned.1.call-done = bf16[2048,2048]{1,0:T(8,128)(2,1)} async-done(((bf16[256,2048]{1,0:T(8,128)(2,1)}), bf16[2048,2048]{1,0:T(8,128)(2,1)}) %all-gather.26.cloned.1.call-update) | async-done | bytes 8388624 | tf_op jit(solution)/shard_map/all_gather | solution.py:186
  536.6 71.0 %all-gather.24.cloned.1.call-done = bf16[1536,2048]{1,0:T(8,128)(2,1)} async-done(((bf16[384,2048]{1,0:T(8,128)(2,1)}), bf16[1536,2048]{1,0:T(8,128)(2,1)}) %all-gather.24.cloned.1.call-update) | async-done | bytes 6291472 | tf_op jit(solution)/shard_map/all_gather | solution.py:81
  607.6 18.9 fusion.84
  626.5 64.7 %all-gather.28.cloned.1.call-done = bf16[2048,2048]{1,0:T(8,128)(2,1)} async-done(((bf16[256,2048]{1,0:T(8,128)(2,1)}), bf16[2048,2048]{1,0:T(8,128)(2,1)}) %all-gather.28.cloned.1.call-update) | async-done | bytes 8388624 | tf_op jit(solution)/shard_map/all_gather | solution.py:187
  691.3 19.0 fusion.85
  710.2 51.9 %all-gather.32.cloned.1.call-done = bf16[1536,2048]{1,0:T(8,128)(2,1)} async-done(((bf16[384,2048]{1,0:T(8,128)(2,1)}), bf16[1536,2048]{1,0:T(8,128)(2,1)}) %all-gather.32.cloned.1.call-update) | async-done | bytes 6291472 | tf_op jit(solution)/shard_map/all_gather | solution.py:81
  762.1 84.1 %all-gather.30.cloned.1.call-done = bf16[2048,2048]{1,0:T(8,128)(2,1)} async-done(((bf16[2048,256]{1,0:T(8,128)(2,1)}), bf16[2048,2048]{1,0:T(8,128)(2,1)}) %all-gather.30.cloned.1.call-update) | async-done | bytes 8388624 | tf_op jit(solution)/shard_map/all_gather | solution.py:188
  846.2 27.1 %multiply_convert_fusion = (bf16[1536,2048]{1,0:T(8,128)(2,1)S(1)}, bf16[1536,2048]{1,0:T(8,128)(2,1)S(1)}, bf16[1536,2048]{1,0:T(8,128)(2,1)}) fusion(f32[1536,2048]{1,0:T(8,128)} %fusion.84, f32[1536,2048]{1,0:T(8,128)} %fusion.85, bf16[1536,2048]{1,0:T(8,128)(2,1)} %all-gather.32.cloned.1.call-done, bf16[2048,2048]{1,0:T(8,128)(2,1)} %all-gather.30.cloned.1.call-done), kind=kOutput, calls=%fused_computation.91 | convolution fusion | flops 12935233536 | bytes 58720256 | tf_op jit(solution)/shard_map/dot_general | solution.py:30
  873.2 19.2 fusion.87
  892.5 20.5 %convolution_add_fusion = f32[1536,2048]{1,0:T(8,128)} fusion(f32[1536,2048]{1,0:T(8,128)} %fusion.87, bf16[1536,2048]{1,0:T(8,128)(2,1)S(1)} %get-tuple-element.496, bf16[2048,2048]{1,0:T(8,128)(2,1)} %all-gather.28.cloned.1.call-done), kind=kOutput, calls=%fused_computation.95 | convolution fusion | flops 12888047616 | bytes 39845888 | tf_op jit(solution)/shard_map/dot_general | solution.py:30
  913.0 19.0 fusion.86
  932.2 99.7 %reduce-scatter.22.cloned.1.call-done = f32[384,2048]{1,0:T(8,128)} async-done(((f32[1536,2048]{1,0:T(8,128)}), f32[384,2048]{1,0:T(8,128)}) %reduce-scatter.22.cloned.1.call-update) | async-done | bytes 3145744 | tf_op jit(solution)/shard_map/reduce_scatter | solution.py:85
  1035.2 120.5 %reduce-scatter.20.cloned.1.call-done = f32[384,2048]{1,0:T(8,128)} async-done(((f32[1536,2048]{1,0:T(8,128)}), f32[384,2048]{1,0:T(8,128)}) %reduce-scatter.20.cloned.1.call-update) | async-done | bytes 3145744 | tf_op jit(solution)/shard_map/reduce_scatter | solution.py:85
  1155.7 5.8 multiply_convert_fusion.3
  1161.6 70.1 %all-gather.34.cloned.1.call-done = bf16[1536,2048]{1,0:T(8,128)(2,1)} async-done(((bf16[384,2048]{1,0:T(8,128)(2,1)}), bf16[1536,2048]{1,0:T(8,128)(2,1)}) %all-gather.34.cloned.1.call-update) | async-done | bytes 6291472 | tf_op jit(solution)/shard_map/all_gather | solution.py:81
  1231.7 6.9 convolution_convert_fusion.5
  1246.0 133.2 %while.33 = (s32[]{:T(128)}, f32[4,384,512]{1,2,0:T(8,128)}, f32[4,1280,2,64]{1,3,2,0:T(8,128)}, bf16[4,1280,2,64]{1,3,2,0:T(8,128)(2,1)}, bf16[4,1024,2,64]{1,3...) while((s32[]{:T(128)}, f32[4,384,512]{1,2,0:T(8,128)}, ...), condition=%wide.region_12.13_spmd, body=%wide.region_10.12_spmd.sunk | while | flops 2560690176 | bytes 206299728 | solution.py:294
  1253.4 8.5 fusion.162
  1262.0 7.1 fusion.163
  1286.8 8.5 fusion.162
  1295.3 7.1 fusion.163
  1320.1 8.5 fusion.162
  1328.6 7.1 fusion.163
  1353.4 8.5 fusion.162
  1361.9 7.1 fusion.163
  1390.1 19.6 convolution_convert_fusion.2
  1409.7 19.7 convolution_convert_fusion.1
  1429.4 19.9 convolution_convert_fusion
  1487.3 5.6 convolution_convert_fusion.7
  1497.9 7.7 convolution_convert_fusion.4
  1505.7 8.2 convolution_convert_fusion.3
  1514.3 8.2 fusion.88
  1524.3 11.6 add_add_fusion
  1543.3 87.4 %reduce-scatter.36.cloned.1.call-done = bf16[256,2048]{1,0:T(8,128)(2,1)} async-done(((bf16[2048,2048]{1,0:T(8,128)(2,1)}), bf16[256,2048]{1,0:T(8,128)(2,1)}) %reduce-scatter.36.cloned.1.call-update) | async-done | bytes 1048592 | tf_op jit(solution)/shard_map/reduce_scatter | solution.py:224
  1633.5 87.5 %reduce-scatter.38.cloned.1.call-done = bf16[2048,256]{1,0:T(8,128)(2,1)} async-done(((bf16[2048,2048]{1,0:T(8,128)(2,1)}), bf16[2048,256]{1,0:T(8,128)(2,1)}) %reduce-scatter.38.cloned.1.call-update) | async-done | bytes 1048592 | tf_op jit(solution)/shard_map/reduce_scatter | solution.py:227
  1723.7 29.2 %reduce-scatter.30.cloned.1.call-done = bf16[256,128]{1,0:T(8,128)(2,1)} async-done(((bf16[2048,128]{1,0:T(8,128)(2,1)}), bf16[256,128]{1,0:T(8,128)(2,1)}) %reduce-scatter.30.cloned.1.call-update) | async-done | bytes 65552 | tf_op jit(solution)/shard_map/reduce_scatter | solution.py:357
  1754.4 30.8 %reduce-scatter.28.cloned.1.call-done = bf16[256,128]{1,0:T(8,128)(2,1)} async-done(((bf16[2048,128]{1,0:T(8,128)(2,1)}), bf16[256,128]{1,0:T(8,128)(2,1)}) %reduce-scatter.28.cloned.1.call-update) | async-done | bytes 65552 | tf_op jit(solution)/shard_map/reduce_scatter | solution.py:354
  1786.7 34.9 %reduce-scatter.26.cloned.1.call-done = bf16[256,512]{1,0:T(8,128)(2,1)} async-done(((bf16[2048,512]{1,0:T(8,128)(2,1)}), bf16[256,512]{1,0:T(8,128)(2,1)}) %reduce-scatter.26.cloned.1.call-update) | async-done | bytes 262160 | tf_op jit(solution)/shard_map/reduce_scatter | solution.py:351
  1823.5 35.2 %reduce-scatter.32.cloned.1.call-done = bf16[512,256]{1,0:T(8,128)(2,1)} async-done(((bf16[512,2048]{1,0:T(8,128)(2,1)}), bf16[512,256]{1,0:T(8,128)(2,1)}) %reduce-scatter.32.cloned.1.call-update) | async-done | bytes 262160 | tf_op jit(solution)/shard_map/reduce_scatter | solution.py:360
  1860.5 120.6 %reduce-scatter.24.cloned.1.call-done = f32[384,2048]{1,0:T(8,128)} async-done(((f32[1536,2048]{1,0:T(8,128)}), f32[384,2048]{1,0:T(8,128)}) %reduce-scatter.24.cloned.1.call-update) | async-done | bytes 3145744 | tf_op jit(solution)/shard_map/reduce_scatter | solution.py:85
  1983.8 16.5 all-reduce.5
  2000.4 8.9 all-reduce.4
  (422 shorter events, 255.1 us)
Async XLA Ops:
  7.2 87.9 %all-gather.14.cloned.1.call-start = ((), (), s32[]{:S(2)}) async-start(), calls=%async_computation.13 | async-start | bytes 7864320 | tf_op jit(solution)/shard_map/all_gather | solution.py:81
  21.4 6.2 copy-start.52
  23.2 7.5 copy-start.31
  26.7 103.1 %all-gather.20.cloned.1.call-start = ((), (), s32[]{:S(2)}) async-start(), calls=%async_computation.16 | async-start | bytes 2359296 | tf_op jit(solution)/shard_map/all_gather | solution.py:121
  27.5 127.2 %all-gather.18.cloned.1.call-start = ((), (), s32[]{:S(2)}) async-start(), calls=%async_computation.15 | async-start | bytes 1179648 | tf_op jit(solution)/shard_map/all_gather | solution.py:155
  27.6 18.0 copy-start.48
  30.7 70.1 %copy-start.14 = (f32[4,384,64]{1,0,2:T(4,128)}, f32[4,384,64]{1,0,2:T(4,128)S(1)}, u32[]{:S(2)}) copy-start(f32[4,384,64]{1,0,2:T(4,128)S(1)} %get-tuple-element.513) | copy-start | bytes 1179652
  45.6 54.5 %copy-start.12 = (bf16[2048,128]{1,0:T(8,128)(2,1)}, bf16[2048,128]{1,0:T(8,128)(2,1)S(1)}, u32[]{:S(2)}) copy-start(bf16[2048,128]{1,0:T(8,128)(2,1)S(1)} %all_gather.58) | copy-start | bytes 1572868
  101.8 77.6 %all-gather.16.cloned.1.call-start = ((), (), s32[]{:S(2)}) async-start(), calls=%async_computation.14 | async-start | bytes 1179648 | tf_op jit(solution)/shard_map/all_gather | solution.py:156
  125.7 196.6 %all-gather.22.cloned.1.call-start = ((), (), s32[]{:S(2)}) async-start(), calls=%async_computation.17 | async-start | bytes 2359296 | tf_op jit(solution)/shard_map/all_gather | solution.py:124
  126.3 326.6 %reduce-scatter.18.cloned.1.call-start = ((), (), s32[]{:S(2)}) async-start(), calls=%async_computation.18 | async-start | bytes 15728640 | tf_op jit(solution)/shard_map/reduce_scatter | solution.py:85
  193.9 8.9 copy-start.10
  226.5 8.7 copy-start.10
  258.9 8.7 copy-start.10
  291.3 8.7 copy-start.10
  322.3 11.1 copy-start.5
  322.3 11.1 copy-start.7
  333.4 119.6 %copy-start.3 = (bf16[384,2048]{1,0:T(8,128)(2,1)S(1)}, bf16[384,2048]{1,0:T(8,128)(2,1)}, u32[]{:S(2)}) copy-start(bf16[384,2048]{1,0:T(8,128)(2,1)} %param.17) | copy-start | bytes 4718596
  333.4 203.2 %all-gather.26.cloned.1.call-start = ((), (), s32[]{:S(2)}) async-start(), calls=%async_computation.20 | async-start | bytes 9437184 | tf_op jit(solution)/shard_map/all_gather | solution.py:186
  334.1 273.4 %all-gather.24.cloned.1.call-start = ((), (), s32[]{:S(2)}) async-start(), calls=%async_computation.19 | async-start | bytes 7864320 | tf_op jit(solution)/shard_map/all_gather | solution.py:81
  344.9 110.5 %copy-start.27 = (f32[8,1,256]{2,1,0:T(1,128)}, f32[8,1,256]{2,1,0:T(1,128)S(1)}, u32[]{:S(2)}) copy-start(f32[8,1,256]{2,1,0:T(1,128)S(1)} %convert_element_type.213) | copy-start | bytes 24580
  458.6 232.7 %all-gather.28.cloned.1.call-start = ((), (), s32[]{:S(2)}) async-start(), calls=%async_computation.21 | async-start | bytes 9437184 | tf_op jit(solution)/shard_map/all_gather | solution.py:187
  459.3 302.7 %all-gather.32.cloned.1.call-start = ((), (), s32[]{:S(2)}) async-start(), calls=%async_computation.24 | async-start | bytes 7864320 | tf_op jit(solution)/shard_map/all_gather | solution.py:81
  459.4 167.1 %copy-start.33 = (s32[1536]{0:T(1024)}, s32[1536]{0:T(1024)S(1)}, u32[]{:S(2)}) copy-start(s32[1536]{0:T(1024)S(1)} %broadcast_in_dim.173) | copy-start | bytes 18436
  459.5 167.1 %copy-start.46 = (pred[1536]{0:T(1024)(128)(4,1)}, pred[1536]{0:T(1024)(128)(4,1)S(1)}, u32[]{:S(2)}) copy-start(pred[1536]{0:T(1024)(128)(4,1)S(1)} %broadcast_in_dim.172) | copy-start | bytes 4612
  459.6 167.0 %copy-start.35 = (s32[1536]{0:T(1024)}, s32[1536]{0:T(1024)S(1)}, u32[]{:S(2)}) copy-start(s32[1536]{0:T(1024)S(1)} %add.237) | copy-start | bytes 18436
  461.9 384.3 %all-gather.30.cloned.1.call-start = ((), (), s32[]{:S(2)}) async-start(), calls=%async_computation.22 | async-start | bytes 9437184 | tf_op jit(solution)/shard_map/all_gather | solution.py:188
  462.6 569.3 %reduce-scatter.22.cloned.1.call-start = ((), (), s32[]{:S(2)}) async-start(), calls=%async_computation.25 | async-start | bytes 15728640 | tf_op jit(solution)/shard_map/reduce_scatter | solution.py:85
  873.2 19.2 copy-start.59
  873.2 19.2 copy-start.58
  913.0 242.7 %reduce-scatter.20.cloned.1.call-start = ((), (), s32[]{:S(2)}) async-start(), calls=%async_computation.23 | async-start | bytes 15728640 | tf_op jit(solution)/shard_map/reduce_scatter | solution.py:85
  932.0 99.9 %copy-start.2 = (f32[384,2048]{1,0:T(8,128)S(1)}, f32[384,2048]{1,0:T(8,128)}, u32[]{:S(2)}) copy-start(f32[384,2048]{1,0:T(8,128)} %copy-done.1) | copy-start | bytes 9437188
  932.0 99.9 %copy-start.28 = (f32[8,1,256]{2,1,0:T(1,128)S(1)}, f32[8,1,256]{2,1,0:T(1,128)}, u32[]{:S(2)}) copy-start(f32[8,1,256]{2,1,0:T(1,128)} %copy-done.27) | copy-start | bytes 24580
  932.0 100.0 %copy-start.38 = (f32[384]{0:T(512)S(1)}, f32[384]{0:T(512)}, u32[]{:S(2)}) copy-start(f32[384]{0:T(512)} %copy-done.37) | copy-start | bytes 4612
  932.0 223.6 %copy-start.44 = (f32[384]{0:T(512)S(1)}, f32[384]{0:T(512)}, u32[]{:S(2)}) copy-start(f32[384]{0:T(512)} %copy-done.43) | copy-start | bytes 4612
  932.0 299.6 %all-gather.34.cloned.1.call-start = ((), (), s32[]{:S(2)}) async-start(), calls=%async_computation.26 | async-start | bytes 7864320 | tf_op jit(solution)/shard_map/all_gather | solution.py:81
  1161.5 313.8 %reduce-scatter.42.cloned.1.call-start = ((), (), s32[]{:S(2)}) async-start(), calls=%async_computation.36 | async-start | bytes 1179648
  1248.0 5.5 copy-start.6
  1269.1 5.8 copy-start
  1281.3 5.5 copy-start.6
  1302.4 5.8 copy-start
  1314.6 5.5 copy-start.6
  1335.7 5.8 copy-start
  1347.9 5.5 copy-start.6
  1369.0 5.8 copy-start
  1384.4 93.7 %reduce-scatter.40.cloned.1.call-start = ((), (), s32[]{:S(2)}) async-start(), calls=%async_computation.35 | async-start | bytes 1179648
  1390.0 150.5 %reduce-scatter.34.cloned.1.call-start = ((), (), s32[]{:S(2)}) async-start(), calls=%async_computation.32 | async-start | bytes 9437184 | tf_op jit(solution)/shard_map/reduce_scatter | solution.py:221
  1409.6 221.1 %reduce-scatter.36.cloned.1.call-start = ((), (), s32[]{:S(2)}) async-start(), calls=%async_computation.33 | async-start | bytes 9437184 | tf_op jit(solution)/shard_map/reduce_scatter | solution.py:224
  1429.4 291.6 %reduce-scatter.38.cloned.1.call-start = ((), (), s32[]{:S(2)}) async-start(), calls=%async_computation.34 | async-start | bytes 9437184 | tf_op jit(solution)/shard_map/reduce_scatter | solution.py:227
  1449.4 303.6 %reduce-scatter.30.cloned.1.call-start = ((), (), s32[]{:S(2)}) async-start(), calls=%async_computation.30 | async-start | bytes 589824 | tf_op jit(solution)/shard_map/reduce_scatter | solution.py:357
  1454.4 7.3 copy-start.8
  1480.3 5.6 copy-start.15
  1486.0 299.2 %reduce-scatter.28.cloned.1.call-start = ((), (), s32[]{:S(2)}) async-start(), calls=%async_computation.29 | async-start | bytes 589824 | tf_op jit(solution)/shard_map/reduce_scatter | solution.py:354
  1487.3 5.7 copy-start.9
  1492.9 328.7 %reduce-scatter.26.cloned.1.call-start = ((), (), s32[]{:S(2)}) async-start(), calls=%async_computation.28 | async-start | bytes 2359296 | tf_op jit(solution)/shard_map/reduce_scatter | solution.py:351
  1505.6 8.6 copy-start.24
  1505.6 353.1 %reduce-scatter.32.cloned.1.call-start = ((), (), s32[]{:S(2)}) async-start(), calls=%async_computation.31 | async-start | bytes 2359296 | tf_op jit(solution)/shard_map/reduce_scatter | solution.py:360
  1513.9 8.5 copy-start.13
  1513.9 8.5 copy-start.17
  1513.9 467.1 %reduce-scatter.24.cloned.1.call-start = ((), (), s32[]{:S(2)}) async-start(), calls=%async_computation.27 | async-start | bytes 15728640 | tf_op jit(solution)/shard_map/reduce_scatter | solution.py:85
  1633.5 347.5 %copy-start.4 = (bf16[384,2048]{1,0:T(8,128)(2,1)S(1)}, bf16[384,2048]{1,0:T(8,128)(2,1)}, u32[]{:S(2)}) copy-start(bf16[384,2048]{1,0:T(8,128)(2,1)} %param.17) | copy-start | bytes 4718596
  1633.5 347.5 %copy-start.30 = (f32[8,1,256]{2,1,0:T(1,128)S(1)}, f32[8,1,256]{2,1,0:T(1,128)}, u32[]{:S(2)}) copy-start(f32[8,1,256]{2,1,0:T(1,128)} %copy-done.29) | copy-start | bytes 24580
  1633.5 347.5 %copy-start.40 = (f32[384]{0:T(512)S(1)}, f32[384]{0:T(512)}, u32[]{:S(2)}) copy-start(f32[384]{0:T(512)} %copy-done.39) | copy-start | bytes 4612
  1786.7 197.1 %copy-start.45 = (bf16[2048]{0:T(1024)(128)(2,1)S(1)}, bf16[2048]{0:T(1024)(128)(2,1)}, u32[]{:S(2)}) copy-start(bf16[2048]{0:T(1024)(128)(2,1)} %get-tuple-element.412) | copy-start | bytes 12292
  (35 other events, 68.3 us)
Sparse Core Ops, SparseCore 0:
  26.9 68.2 all-gather.13
  96.7 33.0 all-gather.19
  132.0 22.6 all-gather.17
  156.7 22.6 all-gather.15
  180.9 29.3 all-gather.21
  333.5 119.3 reduce-scatter.17
  454.5 82.0 all-gather.25
  539.0 68.5 all-gather.23
  609.2 82.0 all-gather.27
  693.5 68.5 all-gather.31
  763.7 82.4 all-gather.29
  913.1 118.7 reduce-scatter.21
  1035.0 120.5 reduce-scatter.19
  1161.6 70.0 all-gather.33
  1384.5 32.6 reduce-scatter.41
  1419.9 30.7 reduce-scatter.39
  1452.9 87.6 reduce-scatter.33
  1542.7 87.9 reduce-scatter.35
  1633.0 87.9 reduce-scatter.37
  1723.1 29.7 reduce-scatter.29
  1755.8 29.4 reduce-scatter.27
  1787.5 34.0 reduce-scatter.25
  1824.0 34.6 reduce-scatter.31
  1861.6 119.3 reduce-scatter.23
where the time goes:
time: 2030 us; the launch traced here: 2020 us
  waiting for transfers between devices  1250 us (62%)
  matrix products  402 us (20%)
  other arithmetic  140 us (7%)
  local copies, waits for them, and re-layouts  120 us (6%)
  blocking collectives  81.9 us (4%)
    reduce_scatter x4, waiting for transfers between devices, reduce_rows(): lax.psum_scatter(row_terms, 'tensor', scatter_dimension=0, tiled=True)  449 us
    all_gather x4, waiting for transfers between devices, gather_rows(): return lax.all_gather(local_rows, 'tensor', axis=0, tiled=True)  242 us
    dot_general x7, matrix products, dot_back(): lax.dot_general(left_mat, right_mat, (((1,), (1,)), ((), ())), preferred_...  95.3 us
    reduce_scatter x1, waiting for transfers between devices, local(): lax.psum_scatter(grad_down.astype(jnp.bfloat16), 'dp', scatter_dimension=...  87.5 us
    reduce_scatter x1, waiting for transfers between devices, local(): lax.psum_scatter(grad_up_w.astype(jnp.bfloat16), 'dp', scatter_dimension=...  87.4 us
    dot_general x7, matrix products, dot_rows(): lax.dot_general(left_mat, right_mat, (((0,), (0,)), ((), ())), preferred_...  86.2 us
    dot_general x7, matrix products, project(): return jnp.dot(left_mat, right_mat, preferred_element_type=jnp.float32)  86.1 us
    all_gather x1, waiting for transfers between devices, local(): lax.all_gather(w_down, 'dp', axis=1, tiled=True)  84.1 us
  transfers between devices with their start and end apart: 24, of which 21 were waited for; matrix products, arithmetic and copies ran while one was open for 20% of the time, Pallas kernels for 0%

commit v1 on v0

v1 whole, which is shorter than its diff:
```python
import jax
import jax.numpy as jnp
from jax import lax
from jax.sharding import PartitionSpec as P

HEAD_SIZE = 64
NG = 4
PROMPT_DEV = 128
CONT = 256


EPS = 1e-05
THETA = 10000000.0
ATTN_SCALE = 0.015625
RESID_SCALE = 0.22
NEG_FILL = -1e30


def project(left_mat, right_mat):
    return jnp.dot(left_mat, right_mat, preferred_element_type=jnp.float32)


def dot_rows(left_mat, right_mat):
    return lax.dot_general(
        left_mat, right_mat, (((0,), (0,)), ((), ())), preferred_element_type=jnp.float32
    )


def dot_back(left_mat, right_mat):
    return lax.dot_general(
        left_mat, right_mat, (((1,), (1,)), ((), ())), preferred_element_type=jnp.float32
    )


def rope_tables(positions, head_width):
    half_width = head_width // 2
    frequency = THETA ** (-(jnp.arange(half_width).astype(jnp.float32) * 2.0) / head_width)
    angles = positions.astype(jnp.float32)[:, None] * frequency[None, :]
    angles = jnp.concatenate([angles, angles], axis=1)
    return (jnp.cos(angles), jnp.sin(angles))


def apply_rotary(values, cosine_table, sine_values):
    half_width = values.shape[-1] // 2
    turned = jnp.concatenate([-values[..., half_width:], values[..., :half_width]], axis=-1)
    return values * cosine_table[:, None, :] + turned * sine_values[:, None, :]


def unrotate(values, cosine_table, sine_values):
    half_width = values.shape[-1] // 2
    scaled_sin = values * sine_values[:, None, :]
    turned = jnp.concatenate([scaled_sin[..., half_width:], -scaled_sin[..., :half_width]], axis=-1)
    return values * cosine_table[:, None, :] + turned


def build_mask(base_row, prompt_length, portion_rows, cont_rows, prompt_row_count):
    row_ids = jnp.arange(portion_rows + cont_rows)[:, None]
    key_ids = jnp.arange(prompt_row_count + cont_rows)[None, :]
    in_prompt = key_ids < prompt_row_count
    prompt_part = in_prompt & (key_ids <= base_row + row_ids)
    cont_part = jnp.where(
        in_prompt, key_ids < prompt_length, key_ids - prompt_row_count <= row_ids - portion_rows
    )
    return jnp.where(row_ids < portion_rows, prompt_part, cont_part)


def norm_parts(values):
    row_scale = lax.rsqrt(jnp.mean(values * values, axis=-1, keepdims=True) + EPS)
    return (values * row_scale, row_scale)


def norm_back(grad_norm, unit_rows, row_scale, gain_vec):
    scaled = grad_norm * gain_vec
    grad_in = row_scale * (
        scaled - unit_rows * jnp.mean(scaled * unit_rows, axis=-1, keepdims=True)
    )
    return (grad_in, jnp.sum(grad_norm * unit_rows, axis=0))


def swap(block, bit):
    pairs = [(i, i ^ bit) for i in range(lax.axis_size("tensor"))]
    return lax.ppermute(block, "tensor", pairs)


def gather_blocks(local_rows):
    if lax.axis_size("tensor") != NG:
        whole = lax.all_gather(local_rows, "tensor", axis=0, tiled=True)
        return jnp.split(whole, NG, axis=0)
    half = local_rows.shape[0] // 2
    one = swap(local_rows, 1)
    two = swap(local_rows, 2)
    top = swap(two[:half], 1)
    low = swap(one[half:], 2)
    return [local_rows, one, two, jnp.concatenate([top, low], axis=0)]


def scatter_blocks(make_block):
    if lax.axis_size("tensor") != NG:
        whole = jnp.concatenate([make_block(k) for k in range(NG)], axis=0)
        return lax.psum_scatter(
            whole.astype(jnp.bfloat16), "tensor", scatter_dimension=0, tiled=True
        ).astype(jnp.float32)
    three = make_block(3).astype(jnp.bfloat16)
    half = three.shape[0] // 2
    top = swap(three[:half], 1)
    low = swap(three[half:], 2)
    one = make_block(1)
    one = jnp.concatenate([one[:half], one[half:] + low.astype(jnp.float32)], axis=0)
    one = swap(one.astype(jnp.bfloat16), 1)
    two = make_block(2)
    two = jnp.concatenate([two[:half] + top.astype(jnp.float32), two[half:]], axis=0)
    two = swap(two.astype(jnp.bfloat16), 2)
    return make_block(0) + one.astype(jnp.float32) + two.astype(jnp.float32)


def gather_dp(piece):
    return lax.all_gather(piece, "dp", axis=0, tiled=True)


def scatter_dp(whole):
    return lax.psum_scatter(
        whole.astype(jnp.bfloat16), "dp", scatter_dimension=0, tiled=True
    ).astype(jnp.float32)


def score_block(single_query, every_key, key_mask):
    score_matrix = (
        jnp.einsum("wclz,icz->clwi", single_query, every_key, preferred_element_type=jnp.float32)
        * ATTN_SCALE
    )
    return jnp.where(key_mask[None, None], score_matrix, NEG_FILL)


FF_PARTS = 2


def local(
    tokens,
    cotangent,
    prompt_len,
    cont_len,
    w_query,
    key_weight,
    value_weight,
    w_out,
    w_gate,
    w_up,
    w_down,
    attn_gain,
    ffn_gain,
):
    portion = PROMPT_DEV
    group_rows = PROMPT_DEV + CONT
    dp_size = lax.axis_size("dp")
    prompt_rows = PROMPT_DEV * dp_size
    dp_index = lax.axis_index("dp")
    tensor_index = lax.axis_index("tensor")
    relative = lax.axis_size("tensor") == NG
    local_rows = tokens.shape[0]
    q_cols = w_query.shape[1]
    kv_cols = key_weight.shape[1]
    head_count = q_cols // HEAD_SIZE
    group_count = kv_cols // HEAD_SIZE
    repeat = head_count // group_count
    qkv_cols = q_cols + 2 * kv_cols
    ff_cols = w_gate.shape[1]
    part = ff_cols // FF_PARTS

    attn_pack = gather_dp(
        jnp.concatenate([w_query, key_weight, value_weight, w_out.T], axis=1)
    )
    full_qkv = attn_pack[:, :qkv_cols]
    full_out_t = attn_pack[:, qkv_cols:]
    down_t = w_down.T
    gate_parts, up_parts, down_parts = [], [], []
    for c in range(FF_PARTS):
        cols = slice(c * part, (c + 1) * part)
        gate_parts.append(gather_dp(w_gate[:, cols]))
        up_parts.append(gather_dp(w_up[:, cols]))
        down_parts.append(gather_dp(down_t[:, cols]))
    gains = gather_dp(jnp.stack([attn_gain, ffn_gain], axis=1)).astype(jnp.float32)
    gain_one = gains[:, 0]
    gain_two = gains[:, 1]

    order = [tensor_index ^ k if relative else k for k in range(NG)]
    lengths = jnp.stack([prompt_len[g] for g in order]) if relative else prompt_len
    col_ids = jnp.arange(group_rows)[None, :]
    starts = lengths[:, None]
    positions = jnp.where(
        col_ids < portion, dp_index * portion + col_ids, starts + col_ids - portion
    ).reshape(-1)
    valid_rows = jnp.where(
        col_ids < portion,
        dp_index * portion + col_ids < prompt_len[:, None],
        col_ids - portion < cont_len,
    ).reshape(-1)
    valid_local = lax.dynamic_slice_in_dim(
        valid_rows.astype(jnp.float32), tensor_index * local_rows, local_rows
    )
    cosine_table, sine_values = rope_tables(positions, HEAD_SIZE)

    resid_in = tokens.astype(jnp.float32)
    unit_one, scale_one = norm_parts(resid_in)
    normed_blocks = gather_blocks((unit_one * gain_one).astype(jnp.bfloat16))
    grad_y = cotangent.astype(jnp.float32) * valid_local[:, None]
    grad_ffn_blocks = gather_blocks((RESID_SCALE * grad_y).astype(jnp.bfloat16))

    normed = jnp.concatenate(normed_blocks, axis=0)
    qkv = project(normed, full_qkv)
    query_rot = apply_rotary(
        qkv[:, :q_cols].reshape(-1, head_count, HEAD_SIZE), cosine_table, sine_values
    ).astype(jnp.bfloat16)
    key_rot = apply_rotary(
        qkv[:, q_cols : q_cols + kv_cols].reshape(-1, group_count, HEAD_SIZE),
        cosine_table,
        sine_values,
    ).astype(jnp.bfloat16)
    query_grp = query_rot.reshape(NG, group_rows, group_count, repeat, HEAD_SIZE)
    kv_grp = jnp.concatenate(
        [key_rot.reshape(-1, kv_cols), qkv[:, q_cols + kv_cols :].astype(jnp.bfloat16)], axis=1
    ).reshape(NG, group_rows, 2 * kv_cols)
    prompt_kv = lax.all_gather(kv_grp[:, :portion], "dp", axis=0)

    def group_setup(k):
        key_mask = build_mask(dp_index * portion, lengths[k], portion, CONT, prompt_rows)
        kv_all = jnp.concatenate(
            [prompt_kv[:, k].reshape(prompt_rows, 2 * kv_cols), kv_grp[k, portion:]], axis=0
        )
        every_key = kv_all[:, :kv_cols].reshape(-1, group_count, HEAD_SIZE)
        every_value = kv_all[:, kv_cols:].reshape(-1, group_count, HEAD_SIZE)
        return key_mask, every_key, every_value

    kept = {}

    def forward_group(k):
        key_mask, every_key, every_value = group_setup(k)
        score_matrix = score_block(query_grp[k], every_key, key_mask)
        row_top = jnp.max(score_matrix, axis=-1, keepdims=True)
        weights = jnp.exp(score_matrix - row_top)
        row_total = jnp.sum(weights, axis=-1, keepdims=True)
        probability = (weights / row_total).astype(jnp.bfloat16)
        mixed = jnp.einsum(
            "yxks,syt->kyxt", probability, every_value, preferred_element_type=jnp.float32
        )
        mixed = mixed.reshape(group_rows, q_cols).astype(jnp.bfloat16)
        kept[k] = (row_top, row_total, mixed)
        return dot_back(mixed, full_out_t)

    hidden = resid_in + RESID_SCALE * scatter_blocks(forward_group)
    unit_two, scale_two = norm_parts(hidden)
    normed_two = jnp.concatenate(
        gather_blocks((unit_two * gain_two).astype(jnp.bfloat16)), axis=0
    )
    grad_ffn = jnp.concatenate(grad_ffn_blocks, axis=0)

    products, grad_gates, grad_ups = [], [], []
    gate_grads, up_grads, down_grads = [], [], []
    for c in range(FF_PARTS):
        gate_val = project(normed_two, gate_parts[c])
        up_val = project(normed_two, up_parts[c])
        sigmoid_gate = jax.nn.sigmoid(gate_val)
        product = (gate_val * sigmoid_gate * up_val).astype(jnp.bfloat16)
        down_grads.append(scatter_dp(dot_rows(grad_ffn, product)))
        grad_prod = project(grad_ffn, down_parts[c])
        grad_gate_val = (
            grad_prod * up_val * sigmoid_gate * (1.0 + gate_val * (1.0 - sigmoid_gate))
        ).astype(jnp.bfloat16)
        grad_up_val = (grad_prod * gate_val * sigmoid_gate).astype(jnp.bfloat16)
        gate_grads.append(scatter_dp(dot_rows(normed_two, grad_gate_val)))
        up_grads.append(scatter_dp(dot_rows(normed_two, grad_up_val)))
        products.append(product)
        grad_gates.append(grad_gate_val)
        grad_ups.append(grad_up_val)

    def rows_of(array, k):
        return array[k * group_rows : (k + 1) * group_rows]

    def ffn_back_block(k):
        total = 0.0
        for c in range(FF_PARTS):
            total = total + dot_back(rows_of(grad_gates[c], k), gate_parts[c])
            total = total + dot_back(rows_of(grad_ups[c], k), up_parts[c])
        return total

    def ffn_out_block(k):
        total = 0.0
        for c in range(FF_PARTS):
            total = total + dot_back(rows_of(products[c], k), down_parts[c])
        return total

    grad_normed_two = scatter_blocks(ffn_back_block)
    output = (hidden + RESID_SCALE * scatter_blocks(ffn_out_block)).astype(jnp.bfloat16)
    grad_hidden_norm, gain_two_part = norm_back(grad_normed_two, unit_two, scale_two, gain_two)
    grad_hidden = grad_y + grad_hidden_norm

    grad_attn_blocks = gather_blocks((RESID_SCALE * grad_hidden).astype(jnp.bfloat16))
    grad_attn = jnp.concatenate(grad_attn_blocks, axis=0)
    mixed_rows = jnp.concatenate([kept[k][2] for k in range(NG)], axis=0)
    grad_out = scatter_dp(dot_rows(grad_attn, mixed_rows)).T

    def backward_group(k):
        key_mask, every_key, every_value = group_setup(k)
        row_top, row_total, _ = kept[k]
        single_query = query_grp[k]
        single_gradient = (
            project(grad_attn_blocks[k], full_out_t)
            .astype(jnp.bfloat16)
            .reshape(group_rows, group_count, repeat, HEAD_SIZE)
        )
        score_matrix = score_block(single_query, every_key, key_mask)
        probability_rows = jnp.exp(score_matrix - row_top) / row_total
        grad_probs = jnp.einsum(
            "wclz,icz->clwi", single_gradient, every_value, preferred_element_type=jnp.float32
        )
        row_inner = jnp.sum(probability_rows * grad_probs, axis=-1, keepdims=True)
        score_gradient = (probability_rows * (grad_probs - row_inner)).astype(jnp.bfloat16)
        grad_query_one = (
            jnp.einsum(
                "yxks,syt->kyxt", score_gradient, every_key, preferred_element_type=jnp.float32
            )
            * ATTN_SCALE
        )
        grad_key_one = (
            jnp.einsum(
                "kjsv,skjb->vkb", score_gradient, single_query, preferred_element_type=jnp.float32
            )
            * ATTN_SCALE
        )
        grad_value_one = jnp.einsum(
            "kjsv,skjb->vkb",
            probability_rows.astype(jnp.bfloat16),
            single_gradient,
            preferred_element_type=jnp.float32,
        )
        grad_kv = jnp.concatenate(
            [grad_key_one.reshape(-1, kv_cols), grad_value_one.reshape(-1, kv_cols)], axis=1
        )
        return grad_query_one, grad_kv

    backs = [backward_group(k) for k in range(NG)]
    prompt_grad = jnp.stack(
        [b[1][:prompt_rows].reshape(dp_size, portion, 2 * kv_cols) for b in backs], axis=1
    ).reshape(dp_size * NG * portion, 2 * kv_cols)
    prompt_grad = scatter_dp(prompt_grad).reshape(NG, portion, 2 * kv_cols)
    kv_grad = jnp.concatenate(
        [prompt_grad, jnp.stack([b[1][prompt_rows:] for b in backs])], axis=1
    ).reshape(NG * group_rows, 2 * kv_cols)
    query_grad = unrotate(
        jnp.stack([b[0] for b in backs]).reshape(-1, head_count, HEAD_SIZE),
        cosine_table,
        sine_values,
    ).reshape(-1, q_cols)
    key_grad = unrotate(
        kv_grad[:, :kv_cols].reshape(-1, group_count, HEAD_SIZE), cosine_table, sine_values
    ).reshape(-1, kv_cols)
    qkv_grad = jnp.concatenate([query_grad, key_grad, kv_grad[:, kv_cols:]], axis=1).astype(
        jnp.bfloat16
    )
    grad_normed = scatter_blocks(lambda k: dot_back(rows_of(qkv_grad, k), full_qkv))
    qkv_w_grad = scatter_dp(dot_rows(normed, qkv_grad))
    grad_input_norm, gain_one_part = norm_back(grad_normed, unit_one, scale_one, gain_one)
    input_grad = grad_hidden + grad_input_norm
    gain_grads = lax.psum_scatter(
        jnp.stack([gain_one_part, gain_two_part], axis=1),
        ("dp", "tensor"),
        scatter_dimension=0,
        tiled=True,
    )
    return (
        output,
        input_grad,
        qkv_w_grad[:, :q_cols],
        qkv_w_grad[:, q_cols : q_cols + kv_cols],
        qkv_w_grad[:, q_cols + kv_cols :],
        grad_out,
        jnp.concatenate(gate_grads, axis=1),
        jnp.concatenate(up_grads, axis=1),
        jnp.concatenate(down_grads, axis=1).T,
        gain_grads[:, 0],
        gain_grads[:, 1],
    )


def solution(mesh):
    placed = (
        P(("dp", "tensor"), None),
        P(("dp", "tensor"), None),
        P(),
        P(None, "dp"),
        P("dp", "tensor"),
        P("dp", "tensor"),
        P("dp", "tensor"),
        P("tensor", "dp"),
        P("dp", "tensor"),
        P("dp", "tensor"),
        P("tensor", "dp"),
        P("dp"),
        P("dp"),
    )
    return jax.shard_map(
        local,
        mesh=mesh,
        in_specs=placed,
        out_specs=(
            P(("dp", "tensor"), None),
            P(("dp", "tensor"), None),
            P("dp", "tensor"),
            P("dp", "tensor"),
            P("dp", "tensor"),
            P("tensor", "dp"),
            P("dp", "tensor"),
            P("dp", "tensor"),
            P("tensor", "dp"),
            P(("dp", "tensor")),
            P(("dp", "tensor")),
        ),
        check_vma=False,
    )
```

time: 2030 us -> 1250 us (0.62)
  waiting for transfers between devices: 1250 us -> 493 us
  blocking collectives: 81.9 us -> 13.5 us
  other arithmetic: 140 us -> 95.2 us
  starting transfers between devices: 1.62 us -> 39.4 us
  matrix products: 402 us -> 439 us
  local copies, waits for them, and re-layouts: 120 us -> 143 us
    reduce_scatter x11 -> x9, waiting for transfers between devices: 755 us -> 152 us  [scatter_dp(): lax.psum_scatter(whole.astype(jnp.bfloat16), 'dp', scatter_dimension=0, t...]
    all_gather x11 -> x8, waiting for transfers between devices: 491 us -> 16.7 us  [the longest x7 16.7 us: gather_dp(): return lax.all_gather(piece, 'dp', axis=0, tiled=True)]
    ppermute x0 -> x32, waiting for transfers between devices: none -> 193 us  [swap(): return lax.ppermute(block, 'tensor', pairs)]
    unnamed x26 -> x19, waiting for transfers between devices: 3.62 us -> 131 us
    dot_general x12 -> x4, matrix products: 96.2 us -> 28.2 us  [forward_group(): jnp.einsum('yxks,syt->kyxt', probability, every_value, preferred_element_...]
    unnamed x126 -> x373, local copies, waits for them, and re-layouts: 20.2 us -> 78.6 us
    all_gather x4 -> x1, blocking collectives: 56.5 us -> 13.5 us  [gather_dp(): return lax.all_gather(piece, 'dp', axis=0, tiled=True)]
    reduce_sum x6 -> x0, other arithmetic: 41.1 us -> none  [the longest x4 35 us: forward_group(): row_total = jnp.sum(weights, axis=-1, keepdims=True)]
  transfers between devices with their start and end apart: 24 -> 50, of which waited for: 21 -> 24; matrix products, arithmetic and copies ran while one was open for 20% -> 41% of each run, Pallas kernels for 0% -> 0%
where the time goes in v1:
time: 1250 us; the launch traced here: 1240 us
  waiting for transfers between devices  493 us (39%)
  matrix products  439 us (35%)
  local copies, waits for them, and re-layouts  143 us (11%)
  other arithmetic  95.2 us (8%)
  starting transfers between devices  39.4 us (3%)
  between operations  17.1 us (1%)
  blocking collectives  13.5 us (1%)
    ppermute x32, waiting for transfers between devices, swap(): return lax.ppermute(block, 'tensor', pairs)  193 us
    reduce_scatter x9, waiting for transfers between devices, scatter_dp(): lax.psum_scatter(whole.astype(jnp.bfloat16), 'dp', scatter_dimension=0, t...  152 us
    unnamed x19, waiting for transfers between devices  131 us
    dot_general x11, matrix products, project(): return jnp.dot(left_mat, right_mat, preferred_element_type=jnp.float32)  106 us
    dot_general x32, matrix products, dot_back(): lax.dot_general(left_mat, right_mat, (((1,), (1,)), ((), ())), preferred_...  99.5 us
    dot_general x8, matrix products, dot_rows(): lax.dot_general(left_mat, right_mat, (((0,), (0,)), ((), ())), preferred_...  84.3 us
    unnamed x373, local copies, waits for them, and re-layouts  78.6 us
    dot_general x4, matrix products, backward_group(): jnp.einsum('wclz,icz->clwi', single_gradient, every_value, preferred_elem...  44.9 us
  transfers between devices with their start and end apart: 50, of which 24 were waited for; matrix products, arithmetic and copies ran while one was open for 41% of the time, Pallas kernels for 0%

profile of v1, /device:TPU:0, one launch (start us, length us, event | category | flops | bytes accessed | tf_op | source)
XLA Modules:
  0.0 1239.3 jit_solution(3433281377689596520)
XLA Ops:
  13.6 13.5 %all_gather.30 = bf16[2048,2]{0,1:T(2,128)(2,1)S(1)} all-gather(bf16[256,2]{0,1:T(2,128)(2,1)S(1)} %pad_maximum_fusion.25), channel_id=1, replica_groups=mesh['dp'=8,'tensor'=4] {'dp'}, dimensions={0}, use_global_device_ids=true | all-gather | bytes 9216 | tf_op jit(solution)/shard_map/all_gather | solution.py:117
  37.4 29.1 %collective-permute-done.1 = bf16[384,2048]{1,0:T(8,128)(2,1)S(1)} collective-permute-done((bf16[384,2048]{1,0:T(8,128)(2,1)}, bf16[384,2048]{1,0:T(8,128)(2,1)S(1)}, u32[]{:S(2)}, u32[]{:S(2)}) %collective-permute-start.1) | collective-permute-done | bytes 1572896 | tf_op jit(solution)/shard_map/ppermute | solution.py:82
  78.6 8.2 collective-permute-done.2
  91.6 8.2 fusion.78
  126.0 3.9 slice.521
  141.5 10.0 fusion.238
  151.6 7.1 fusion.117
  164.5 10.2 fusion.239
  174.7 7.0 fusion.114
  188.6 8.6 fusion.241
  197.2 7.1 fusion.111
  209.0 10.2 fusion.240
  225.6 7.0 fusion.108
  235.4 19.5 %collective-permute-done.7 = bf16[384,2048]{1,0:T(8,128)(2,1)S(1)} collective-permute-done((bf16[384,2048]{1,0:T(8,128)(2,1)S(1)}, bf16[384,2048]{1,0:T(8,128)(2,1)S(1)}, u32[]{:S(2)}, u32[]{:S(2)}) %collective-permute-start.7) | collective-permute-done | bytes 1572896 | tf_op jit(solution)/shard_map/ppermute | solution.py:82
  275.5 23.6 %collective-permute-done.9 = bf16[384,2048]{1,0:T(8,128)(2,1)S(1)} collective-permute-done((bf16[384,2048]{1,0:T(8,128)(2,1)}, bf16[384,2048]{1,0:T(8,128)(2,1)S(1)}, u32[]{:S(2)}, u32[]{:S(2)}) %collective-permute-start.9) | collective-permute-done | bytes 1572896 | tf_op jit(solution)/shard_map/ppermute | solution.py:82
  300.6 16.1 %collective-permute-done.18 = bf16[192,2048]{1,0:T(8,128)(2,1)} collective-permute-done((bf16[192,2048]{1,0:T(8,128)(2,1)}, bf16[192,2048]{1,0:T(8,128)(2,1)}, u32[]{:S(2)}, u32[]{:S(2)}) %collective-permute-start.18) | collective-permute-done | bytes 786464 | tf_op jit(solution)/shard_map/ppermute | solution.py:82
  331.8 11.9 fusion.244
  343.7 11.7 fusion.245
  355.4 17.4 %multiply_convert_fusion = (bf16[1536,1024]{1,0:T(8,128)(2,1)S(1)}, bf16[1536,1024]{1,0:T(8,128)(2,1)S(1)}, bf16[1536,1024]{1,0:T(8,128)(2,1)}) fusion(f32[1536,1024]{1,0:T(8,128)} %fusion.244, f32[1536,1024]{1,0:T(8,128)} %fusion.245, bf16[1536,2048]{1,0:T(8,128)(2,1)} %constant_dynamic-update-slice_fusion.10, ...), kind=kOutput, calls=%fused_computation.52 | convolution fusion | flops 6467616768 | bytes 32505856 | tf_op jit(solution)/shard_map/dot_general | solution.py:20
  374.5 3.5 fusion.129
  378.0 12.2 fusion.242
  390.3 11.6 fusion.243
  401.9 16.7 %all-gather.16.cloned.1.call-done = bf16[2048,1024]{0,1:T(8,128)(2,1)} async-done(((bf16[256,1024]{0,1:T(8,128)(2,1)}), bf16[2048,1024]{0,1:T(8,128)(2,1)}) %all-gather.16.cloned.1.call-update) | async-done | bytes 4194320 | tf_op jit(solution)/shard_map/all_gather | solution.py:117
  418.5 18.6 %multiply_convert_fusion.2 = (bf16[1536,1024]{1,0:T(8,128)(2,1)}, bf16[1536,1024]{1,0:T(8,128)(2,1)}, bf16[1536,1024]{1,0:T(8,128)(2,1)}) fusion(f32[1536,1024]{1,0:T(8,128)} %fusion.242, f32[1536,1024]{1,0:T(8,128)} %fusion.243, bf16[1536,2048]{1,0:T(8,128)(2,1)} %constant_dynamic-update-slice_fusion.10, bf16[2048,1024]{0,1:T(8,128)(2,1)} %all-gather.16.cloned.1.call-done), kind=kOutput, calls=%fused_computation.54 | convolution fusion | flops 6467616768 | bytes 32505856 | tf_op jit(solution)/shard_map/dot_general | solution.py:20
  460.2 4.4 fusion.143
  472.9 4.0 collective-permute-done.22
  486.9 4.8 fusion.152
  491.6 21.4 %collective-permute-done.23 = bf16[384,2048]{1,0:T(8,128)(2,1)S(1)} collective-permute-done((bf16[384,2048]{1,0:T(8,128)(2,1)S(1)}, bf16[384,2048]{1,0:T(8,128)(2,1)S(1)}, u32[]{:S(2)}, u32[]{:S(2)}) %collective-permute-start.23) | collective-permute-done | bytes 1572896 | tf_op jit(solution)/shard_map/ppermute | solution.py:82
  514.8 7.0 multiply_reduce_fusion
  521.8 3.9 constant_dynamic-update-slice_fusion.19
  531.4 12.4 fusion.13
  546.9 6.9 fusion.15
  564.0 4.0 convolution_convert_fusion.10
  569.2 13.1 %fusion.7 = (f32[2,4,384]{2,1,0:T(4,128)}, f32[2,1280,384,4]{2,1,3,0:T(8,128)}) fusion(f32[2,4,384,1280]{2,3,1,0:T(8,128)} %get-tuple-element.124, f32[2,4,384]{2,1,0:T(4,128)S(1)} %copy-done.115, bf16[1280,2,64,1]{0,2,3,1:T(8,128)(2,1)} %bitcast.486, bf16[384,2,4,64]{0,3,2,1:T(8,128)(2,1)S(1)} %bitcast.472), kind=kOutput, calls=%fused_computation.11 | convolution fusion | flops 515109888 | bytes 32202752 | tf_op jit(solution)/shard_map/wclz,icz->clwi/dot_general | solution.py:312
  590.6 7.4 fusion.44
  598.1 12.8 %fusion.10 = (f32[2,4,384]{2,1,0:T(4,128)}, f32[2,1280,384,4]{2,1,3,0:T(8,128)}) fusion(f32[2,4,384,1280]{2,3,1,0:T(8,128)} %get-tuple-element.130, f32[2,4,384]{2,1,0:T(4,128)S(1)} %copy-done.117, bf16[1280,2,64,1]{0,2,3,1:T(8,128)(2,1)S(1)} %bitcast.489, bf16[384,2,4,64]{0,3,2,1:T(8,128)(2,1)S(1)} %bitcast.475), kind=kOutput, calls=%fused_computation.16 | convolution fusion | flops 515109888 | bytes 32202752 | tf_op jit(solution)/shard_map/wclz,icz->clwi/dot_general | solution.py:312
  615.1 6.9 fusion.9
  627.2 10.9 fusion.12
  644.0 4.0 fusion.105
  649.2 8.0 fusion.40
  658.3 6.7 fusion.4
  665.0 6.7 fusion.6
  678.2 11.3 convolution_convert_fusion
  691.5 11.2 convolution_convert_fusion.1
  704.6 11.2 convolution_convert_fusion.4
  717.7 11.7 convolution_convert_fusion.5
  731.3 11.2 convolution_convert_fusion.2
  744.5 11.2 convolution_convert_fusion.3
  756.3 4.5 fusion.157
  800.5 7.9 convolution_convert_fusion.7
  819.9 11.1 collective-permute-done.30
  832.7 4.3 collective-permute-done.28
  850.9 19.8 %collective-permute-done.31 = bf16[384,2048]{1,0:T(8,128)(2,1)S(1)} collective-permute-done((bf16[384,2048]{1,0:T(8,128)(2,1)S(1)}, bf16[384,2048]{1,0:T(8,128)(2,1)S(1)}, u32[]{:S(2)}, u32[]{:S(2)}) %collective-permute-start.31) | collective-permute-done | bytes 1572896 | tf_op jit(solution)/shard_map/ppermute | solution.py:82
  870.8 4.0 collective-permute-done.29
  874.8 4.1 fusion.57
  881.8 8.5 convolution_convert_fusion.6
  898.6 19.7 %collective-permute-done.15 = bf16[384,2048]{1,0:T(8,128)(2,1)S(1)} collective-permute-done((bf16[384,2048]{1,0:T(8,128)(2,1)S(1)}, bf16[384,2048]{1,0:T(8,128)(2,1)S(1)}, u32[]{:S(2)}, u32[]{:S(2)}) %collective-permute-start.15) | collective-permute-done | bytes 1572896 | tf_op jit(solution)/shard_map/ppermute | solution.py:82
  921.4 4.7 add_convert_fusion.1
  934.5 30.9 %reduce-scatter.25.cloned.1.call-done = bf16[256,1024]{1,0:T(8,128)(2,1)} async-done(((bf16[2048,1024]{1,0:T(8,128)(2,1)}), bf16[256,1024]{1,0:T(8,128)(2,1)}) %reduce-scatter.25.cloned.1.call-update) | async-done | bytes 524304 | tf_op jit(solution)/shard_map/reduce_scatter | solution.py:121
  965.5 50.6 %reduce-scatter.23.cloned.1.call-done = bf16[256,1024]{1,0:T(8,128)(2,1)} async-done(((bf16[2048,1024]{1,0:T(8,128)(2,1)}), bf16[256,1024]{1,0:T(8,128)(2,1)}) %reduce-scatter.23.cloned.1.call-update) | async-done | bytes 524304 | tf_op jit(solution)/shard_map/reduce_scatter | solution.py:121
  1018.8 34.1 %reduce-scatter.17.cloned.1.call-done = bf16[256,512]{1,0:T(8,128)(2,1)} async-done(((bf16[2048,512]{1,0:T(8,128)(2,1)}), bf16[256,512]{1,0:T(8,128)(2,1)}) %reduce-scatter.17.cloned.1.call-update) | async-done | bytes 262160 | tf_op jit(solution)/shard_map/reduce_scatter | solution.py:121
  1054.9 5.3 fusion.56
  1060.2 129.8 %reduce-scatter.31.cloned.1.call-done = f32[64,2]{1,0:T(8,128)} async-done(((f32[2048,2]{1,0:T(8,128)}), f32[64,2]{1,0:T(8,128)}) %reduce-scatter.31.cloned.1.call-update) | async-done | bytes 528
  1192.1 36.8 %reduce-scatter.15.cloned.1.call-done = bf16[256,768]{1,0:T(8,128)(2,1)} async-done(((bf16[2048,768]{1,0:T(8,128)(2,1)}), bf16[256,768]{1,0:T(8,128)(2,1)}) %reduce-scatter.15.cloned.1.call-update) | async-done | bytes 393232 | tf_op jit(solution)/shard_map/reduce_scatter | solution.py:121
  (670 shorter events, 340.2 us)
Async XLA Ops:
  7.2 84.4 %all-gather.10.cloned.1.call-start = ((), (), s32[]{:S(2)}) async-start(), calls=%async_computation.10 | async-start | bytes 5898240 | tf_op jit(solution)/shard_map/all_gather | solution.py:117
  12.2 125.8 %all-gather.24.cloned.1.call-start = ((), (), s32[]{:S(2)}) async-start(), calls=%async_computation.26 | async-start | bytes 2359296 | tf_op jit(solution)/shard_map/all_gather | solution.py:222
  27.5 231.6 %copy-start.97 = (f32[2048,1]{0,1:T(1,128)}, f32[2048,1]{0,1:T(1,128)S(1)}, u32[]{:S(2)}) copy-start(f32[2048,1]{0,1:T(1,128)S(1)} %get-tuple-element.117) | copy-start | bytes 24580
  29.6 36.9 %collective-permute-start.1 = (bf16[384,2048]{1,0:T(8,128)(2,1)}, bf16[384,2048]{1,0:T(8,128)(2,1)S(1)}, u32[]{:S(2)}, u32[]{:S(2)}) collective-permute-start(bf16[384,2048]{1,0:T(8,128)(2,1)} %get-tuple-element.58), channel_id=1, source_target_pairs={{0,2},{1,3},{2,0},{3,1},{4,6},{5,7},{6,4},{7,5},{8,10},{9,11},{10,... | collective-permute-start | bytes 4718600 | tf_op jit(solution)/shard_map/ppermute | solution.py:82
  31.1 37.8 %collective-permute-start = (bf16[384,2048]{1,0:T(8,128)(2,1)}, bf16[384,2048]{1,0:T(8,128)(2,1)S(1)}, u32[]{:S(2)}, u32[]{:S(2)}) collective-permute-start(bf16[384,2048]{1,0:T(8,128)(2,1)} %get-tuple-element.58), channel_id=1, source_target_pairs={{0,1},{1,0},{2,3},{3,2},{4,5},{5,4},{6,7},{7,6},{8,9},{9,8},{10,11... | collective-permute-start | bytes 4718600 | tf_op jit(solution)/shard_map/ppermute | solution.py:82
  32.7 37.4 %copy-start.122 = (pred[1536]{0:T(1024)(128)(4,1)}, pred[1536]{0:T(1024)(128)(4,1)S(1)}, u32[]{:S(2)}) copy-start(pred[1536]{0:T(1024)(128)(4,1)S(1)} %broadcast_in_dim.228) | copy-start | bytes 4612
  67.4 19.4 %collective-permute-start.2 = (bf16[192,2048]{1,0:T(8,128)(2,1)}, bf16[192,2048]{1,0:T(8,128)(2,1)}, u32[]{:S(2)}, u32[]{:S(2)}) collective-permute-start(bf16[192,2048]{1,0:T(8,128)(2,1)} %slice.507), channel_id=1, source_target_pairs={{0,1},{1,0},{2,3},{3,2},{4,5},{5,4},{6,7},{7,6},{8,9},{9,8},{10,11... | collective-permute-start | bytes 2359304 | tf_op jit(solution)/shard_map/ppermute | solution.py:82
  70.4 19.1 %collective-permute-start.3 = (bf16[192,2048]{1,0:T(8,128)(2,1)}, bf16[192,2048]{1,0:T(8,128)(2,1)}, u32[]{:S(2)}, u32[]{:S(2)}) collective-permute-start(bf16[192,2048]{1,0:T(8,128)(2,1)} %slice.508), channel_id=1, source_target_pairs={{0,2},{1,3},{2,0},{3,1},{4,6},{5,7},{6,4},{7,5},{8,10},{9,11},{10,... | collective-permute-start | bytes 2359304 | tf_op jit(solution)/shard_map/ppermute | solution.py:82
  73.3 29.0 %copy-start.14 = (f32[1536,64]{0,1:T(8,128)}, f32[1536,64]{0,1:T(8,128)S(1)}, u32[]{:S(2)}) copy-start(f32[1536,64]{0,1:T(8,128)S(1)} %get-tuple-element.110) | copy-start | bytes 1179652
  73.3 60.0 %copy-start.12 = (f32[1536,64]{0,1:T(8,128)}, f32[1536,64]{0,1:T(8,128)S(1)}, u32[]{:S(2)}) copy-start(f32[1536,64]{0,1:T(8,128)S(1)} %get-tuple-element.109) | copy-start | bytes 1179652
  105.8 226.0 %all-gather.18.cloned.1.call-start = ((), (), s32[]{:S(2)}) async-start(), calls=%async_computation.14 | async-start | bytes 4718592 | tf_op jit(solution)/shard_map/all_gather | solution.py:117
  108.1 235.6 %all-gather.20.cloned.1.call-start = ((), (), s32[]{:S(2)}) async-start(), calls=%async_computation.15 | async-start | bytes 4718592 | tf_op jit(solution)/shard_map/all_gather | solution.py:117
  110.6 244.8 %all-gather.22.cloned.1.call-start = ((), (), s32[]{:S(2)}) async-start(), calls=%async_computation.16 | async-start | bytes 4718592 | tf_op jit(solution)/shard_map/all_gather | solution.py:117
  112.9 265.1 %all-gather.12.cloned.1.call-start = ((), (), s32[]{:S(2)}) async-start(), calls=%async_computation.11 | async-start | bytes 4718592 | tf_op jit(solution)/shard_map/all_gather | solution.py:117
  113.5 276.7 %all-gather.14.cloned.1.call-start = ((), (), s32[]{:S(2)}) async-start(), calls=%async_computation.12 | async-start | bytes 4718592 | tf_op jit(solution)/shard_map/all_gather | solution.py:117
  116.7 149.6 %collective-permute-start.16 = (bf16[384,2048]{1,0:T(8,128)(2,1)}, bf16[384,2048]{1,0:T(8,128)(2,1)}, u32[]{:S(2)}, u32[]{:S(2)}) collective-permute-start(bf16[384,2048]{1,0:T(8,128)(2,1)} %get-tuple-element.52), channel_id=1, source_target_pairs={{0,1},{1,0},{2,3},{3,2},{4,5},{5,4},{6,7},{7,6},{8,9},{9,8},{10,11... | collective-permute-start | bytes 4718600 | tf_op jit(solution)/shard_map/ppermute | solution.py:82
  117.6 145.7 %collective-permute-start.17 = (bf16[384,2048]{1,0:T(8,128)(2,1)}, bf16[384,2048]{1,0:T(8,128)(2,1)}, u32[]{:S(2)}, u32[]{:S(2)}) collective-permute-start(bf16[384,2048]{1,0:T(8,128)(2,1)} %get-tuple-element.52), channel_id=1, source_target_pairs={{0,2},{1,3},{2,0},{3,1},{4,6},{5,7},{6,4},{7,5},{8,10},{9,11},{10,... | collective-permute-start | bytes 4718600 | tf_op jit(solution)/shard_map/ppermute | solution.py:82
  119.1 299.4 %all-gather.16.cloned.1.call-start = ((), (), s32[]{:S(2)}) async-start(), calls=%async_computation.13 | async-start | bytes 4718592 | tf_op jit(solution)/shard_map/all_gather | solution.py:117
  136.1 28.3 %copy-start.54 = (bf16[384,8,64]{0,2,1:T(8,128)(2,1)}, bf16[384,8,64]{0,2,1:T(8,128)(2,1)S(1)}, u32[]{:S(2)}) copy-start(bf16[384,8,64]{0,2,1:T(8,128)(2,1)S(1)} %get-tuple-element.83) | copy-start | bytes 1179652
  136.1 52.5 %copy-start.56 = (bf16[384,8,64]{0,2,1:T(8,128)(2,1)}, bf16[384,8,64]{0,2,1:T(8,128)(2,1)S(1)}, u32[]{:S(2)}) copy-start(bf16[384,8,64]{0,2,1:T(8,128)(2,1)S(1)} %get-tuple-element.81) | copy-start | bytes 1179652
  185.8 33.5 %collective-permute-start.6 = (bf16[192,2048]{1,0:T(8,128)(2,1)}, bf16[192,2048]{1,0:T(8,128)(2,1)}, u32[]{:S(2)}, u32[]{:S(2)}) collective-permute-start(bf16[192,2048]{1,0:T(8,128)(2,1)} %get-tuple-element.80), channel_id=1, source_target_pairs={{0,1},{1,0},{2,3},{3,2},{4,5},{5,4},{6,7},{7,6},{8,9},{9,8},{10,11... | collective-permute-start | bytes 2359304 | tf_op jit(solution)/shard_map/ppermute | solution.py:82
  188.0 35.0 %collective-permute-start.4 = (bf16[192,2048]{1,0:T(8,128)(2,1)}, bf16[192,2048]{1,0:T(8,128)(2,1)}, u32[]{:S(2)}, u32[]{:S(2)}) collective-permute-start(bf16[192,2048]{1,0:T(8,128)(2,1)} %get-tuple-element.79), channel_id=1, source_target_pairs={{0,2},{1,3},{2,0},{3,1},{4,6},{5,7},{6,4},{7,5},{8,10},{9,11},{10,... | collective-permute-start | bytes 2359304 | tf_op jit(solution)/shard_map/ppermute | solution.py:82
  221.4 33.6 %collective-permute-start.7 = (bf16[384,2048]{1,0:T(8,128)(2,1)S(1)}, bf16[384,2048]{1,0:T(8,128)(2,1)S(1)}, u32[]{:S(2)}, u32[]{:S(2)}) collective-permute-start(bf16[384,2048]{1,0:T(8,128)(2,1)S(1)} %pad_maximum_fusion.5), channel_id=1, source_target_pairs={{0,2},{1,3},{2,0},{3,1},{4,6},{5,7},{6,4},{7,5},{8,10},{9,11},{10,... | collective-permute-start | bytes 4718600 | tf_op jit(solution)/shard_map/ppermute | solution.py:82
  224.5 33.3 %collective-permute-start.5 = (bf16[384,2048]{1,0:T(8,128)(2,1)S(1)}, bf16[384,2048]{1,0:T(8,128)(2,1)S(1)}, u32[]{:S(2)}, u32[]{:S(2)}) collective-permute-start(bf16[384,2048]{1,0:T(8,128)(2,1)S(1)} %pad_maximum_fusion.4), channel_id=1, source_target_pairs={{0,1},{1,0},{2,3},{3,2},{4,5},{5,4},{6,7},{7,6},{8,9},{9,8},{10,11... | collective-permute-start | bytes 4718600 | tf_op jit(solution)/shard_map/ppermute | solution.py:82
  261.7 37.5 %collective-permute-start.9 = (bf16[384,2048]{1,0:T(8,128)(2,1)}, bf16[384,2048]{1,0:T(8,128)(2,1)S(1)}, u32[]{:S(2)}, u32[]{:S(2)}) collective-permute-start(bf16[384,2048]{1,0:T(8,128)(2,1)} %get-tuple-element.54), channel_id=1, source_target_pairs={{0,2},{1,3},{2,0},{3,1},{4,6},{5,7},{6,4},{7,5},{8,10},{9,11},{10,... | collective-permute-start | bytes 4718600 | tf_op jit(solution)/shard_map/ppermute | solution.py:82
  262.2 56.5 %collective-permute-start.8 = (bf16[384,2048]{1,0:T(8,128)(2,1)}, bf16[384,2048]{1,0:T(8,128)(2,1)S(1)}, u32[]{:S(2)}, u32[]{:S(2)}) collective-permute-start(bf16[384,2048]{1,0:T(8,128)(2,1)} %get-tuple-element.54), channel_id=1, source_target_pairs={{0,1},{1,0},{2,3},{3,2},{4,5},{5,4},{6,7},{7,6},{8,9},{9,8},{10,11... | collective-permute-start | bytes 4718600 | tf_op jit(solution)/shard_map/ppermute | solution.py:82
  265.4 51.2 %collective-permute-start.18 = (bf16[192,2048]{1,0:T(8,128)(2,1)}, bf16[192,2048]{1,0:T(8,128)(2,1)}, u32[]{:S(2)}, u32[]{:S(2)}) collective-permute-start(bf16[192,2048]{1,0:T(8,128)(2,1)} %slice.567), channel_id=1, source_target_pairs={{0,1},{1,0},{2,3},{3,2},{4,5},{5,4},{6,7},{7,6},{8,9},{9,8},{10,11... | collective-permute-start | bytes 2359304 | tf_op jit(solution)/shard_map/ppermute | solution.py:82
  268.4 52.0 %collective-permute-start.19 = (bf16[192,2048]{1,0:T(8,128)(2,1)}, bf16[192,2048]{1,0:T(8,128)(2,1)}, u32[]{:S(2)}, u32[]{:S(2)}) collective-permute-start(bf16[192,2048]{1,0:T(8,128)(2,1)} %slice.568), channel_id=1, source_target_pairs={{0,2},{1,3},{2,0},{3,1},{4,6},{5,7},{6,4},{7,5},{8,10},{9,11},{10,... | collective-permute-start | bytes 2359304 | tf_op jit(solution)/shard_map/ppermute | solution.py:82
  270.0 538.5 %reduce-scatter.13.cloned.1.call-start = ((), (), s32[]{:S(2)}) async-start(), calls=%async_computation.17 | async-start | bytes 2359296 | tf_op jit(solution)/shard_map/reduce_scatter | solution.py:121
  299.2 29.1 %collective-permute-start.10 = (bf16[192,2048]{1,0:T(8,128)(2,1)S(1)}, bf16[192,2048]{1,0:T(8,128)(2,1)S(1)}, u32[]{:S(2)}, u32[]{:S(2)}) collective-permute-start(bf16[192,2048]{1,0:T(8,128)(2,1)S(1)} %slice.549), channel_id=1, source_target_pairs={{0,1},{1,0},{2,3},{3,2},{4,5},{5,4},{6,7},{7,6},{8,9},{9,8},{10,11... | collective-permute-start | bytes 2359304 | tf_op jit(solution)/shard_map/ppermute | solution.py:82
  318.8 12.1 collective-permute-start.11
  372.8 142.0 %copy-start.31 = (bf16[1536,1024]{1,0:T(8,128)(2,1)}, bf16[1536,1024]{1,0:T(8,128)(2,1)S(1)}, u32[]{:S(2)}) copy-start(bf16[1536,1024]{1,0:T(8,128)(2,1)S(1)} %get-tuple-element.59) | copy-start | bytes 9437188
  457.2 19.8 %collective-permute-start.22 = (bf16[192,2048]{1,0:T(8,128)(2,1)S(1)}, bf16[192,2048]{1,0:T(8,128)(2,1)S(1)}, u32[]{:S(2)}, u32[]{:S(2)}) collective-permute-start(bf16[192,2048]{1,0:T(8,128)(2,1)S(1)} %get-tuple-element.76), channel_id=1, source_target_pairs={{0,1},{1,0},{2,3},{3,2},{4,5},{5,4},{6,7},{7,6},{8,9},{9,8},{10,11... | collective-permute-start | bytes 2359304 | tf_op jit(solution)/shard_map/ppermute | solution.py:82
  458.7 20.1 %collective-permute-start.20 = (bf16[192,2048]{1,0:T(8,128)(2,1)S(1)}, bf16[192,2048]{1,0:T(8,128)(2,1)S(1)}, u32[]{:S(2)}, u32[]{:S(2)}) collective-permute-start(bf16[192,2048]{1,0:T(8,128)(2,1)S(1)} %get-tuple-element.75), channel_id=1, source_target_pairs={{0,2},{1,3},{2,0},{3,1},{4,6},{5,7},{6,4},{7,5},{8,10},{9,11},{10,... | collective-permute-start | bytes 2359304 | tf_op jit(solution)/shard_map/ppermute | solution.py:82
  477.3 35.8 %collective-permute-start.23 = (bf16[384,2048]{1,0:T(8,128)(2,1)S(1)}, bf16[384,2048]{1,0:T(8,128)(2,1)S(1)}, u32[]{:S(2)}, u32[]{:S(2)}) collective-permute-start(bf16[384,2048]{1,0:T(8,128)(2,1)S(1)} %pad_maximum_fusion.9), channel_id=1, source_target_pairs={{0,2},{1,3},{2,0},{3,1},{4,6},{5,7},{6,4},{7,5},{8,10},{9,11},{10,... | collective-permute-start | bytes 4718600 | tf_op jit(solution)/shard_map/ppermute | solution.py:82
  479.2 35.6 %collective-permute-start.21 = (bf16[384,2048]{1,0:T(8,128)(2,1)S(1)}, bf16[384,2048]{1,0:T(8,128)(2,1)}, u32[]{:S(2)}, u32[]{:S(2)}) collective-permute-start(bf16[384,2048]{1,0:T(8,128)(2,1)S(1)} %pad_maximum_fusion.8), channel_id=1, source_target_pairs={{0,1},{1,0},{2,3},{3,2},{4,5},{5,4},{6,7},{7,6},{8,9},{9,8},{10,11... | collective-permute-start | bytes 4718600 | tf_op jit(solution)/shard_map/ppermute | solution.py:82
  491.6 30.2 %copy-start.19 = (bf16[384,2048]{1,0:T(8,128)(2,1)S(1)}, bf16[384,2048]{1,0:T(8,128)(2,1)}, u32[]{:S(2)}) copy-start(bf16[384,2048]{1,0:T(8,128)(2,1)} %param.14) | copy-start | bytes 4718596
  491.6 30.2 %copy-start.110 = (f32[384]{0:T(512)S(1)}, f32[384]{0:T(512)}, u32[]{:S(2)}) copy-start(f32[384]{0:T(512)} %copy-done.109) | copy-start | bytes 4612
  525.7 61.6 %collective-permute-start.24 = (bf16[384,2048]{1,0:T(8,128)(2,1)}, bf16[384,2048]{1,0:T(8,128)(2,1)}, u32[]{:S(2)}, u32[]{:S(2)}) collective-permute-start(bf16[384,2048]{1,0:T(8,128)(2,1)} %get-tuple-element.49), channel_id=1, source_target_pairs={{0,1},{1,0},{2,3},{3,2},{4,5},{5,4},{6,7},{7,6},{8,9},{9,8},{10,11... | collective-permute-start | bytes 4718600 | tf_op jit(solution)/shard_map/ppermute | solution.py:82
  527.1 36.9 %collective-permute-start.25 = (bf16[384,2048]{1,0:T(8,128)(2,1)}, bf16[384,2048]{1,0:T(8,128)(2,1)}, u32[]{:S(2)}, u32[]{:S(2)}) collective-permute-start(bf16[384,2048]{1,0:T(8,128)(2,1)} %get-tuple-element.49), channel_id=1, source_target_pairs={{0,2},{1,3},{2,0},{3,1},{4,6},{5,7},{6,4},{7,5},{8,10},{9,11},{10,... | collective-permute-start | bytes 4718600 | tf_op jit(solution)/shard_map/ppermute | solution.py:82
  598.1 43.1 %copy-start.43 = (f32[2,64,1280,1]{2,1,3,0:T(8,128)}, f32[2,64,1280,1]{2,1,3,0:T(8,128)S(1)}, u32[]{:S(2)}) copy-start(f32[2,64,1280,1]{2,1,3,0:T(8,128)S(1)} %fusion.44) | copy-start | bytes 1966084
  612.1 31.0 %collective-permute-start.27 = (bf16[192,2048]{1,0:T(8,128)(2,1)S(1)}, bf16[192,2048]{1,0:T(8,128)(2,1)S(1)}, u32[]{:S(2)}, u32[]{:S(2)}) collective-permute-start(bf16[192,2048]{1,0:T(8,128)(2,1)S(1)} %slice.592), channel_id=1, source_target_pairs={{0,2},{1,3},{2,0},{3,1},{4,6},{5,7},{6,4},{7,5},{8,10},{9,11},{10,... | collective-permute-start | bytes 2359304 | tf_op jit(solution)/shard_map/ppermute | solution.py:82
  614.4 29.6 %collective-permute-start.26 = (bf16[192,2048]{1,0:T(8,128)(2,1)S(1)}, bf16[192,2048]{1,0:T(8,128)(2,1)}, u32[]{:S(2)}, u32[]{:S(2)}) collective-permute-start(bf16[192,2048]{1,0:T(8,128)(2,1)S(1)} %slice.591), channel_id=1, source_target_pairs={{0,1},{1,0},{2,3},{3,2},{4,5},{5,4},{6,7},{7,6},{8,9},{9,8},{10,11... | collective-permute-start | bytes 2359304 | tf_op jit(solution)/shard_map/ppermute | solution.py:82
  678.1 248.0 %reduce-scatter.29.cloned.1.call-start = ((), (), s32[]{:S(2)}) async-start(), calls=%async_computation.25 | async-start | bytes 4718592 | tf_op jit(solution)/shard_map/reduce_scatter | solution.py:121
  689.6 236.6 %reduce-scatter.27.cloned.1.call-start = ((), (), s32[]{:S(2)}) async-start(), calls=%async_computation.24 | async-start | bytes 4718592 | tf_op jit(solution)/shard_map/reduce_scatter | solution.py:121
  702.7 229.1 %reduce-scatter.21.cloned.1.call-start = ((), (), s32[]{:S(2)}) async-start(), calls=%async_computation.21 | async-start | bytes 4718592 | tf_op jit(solution)/shard_map/reduce_scatter | solution.py:121
  715.8 216.0 %reduce-scatter.19.cloned.1.call-start = ((), (), s32[]{:S(2)}) async-start(), calls=%async_computation.20 | async-start | bytes 4718592 | tf_op jit(solution)/shard_map/reduce_scatter | solution.py:121
  729.4 236.0 %reduce-scatter.25.cloned.1.call-start = ((), (), s32[]{:S(2)}) async-start(), calls=%async_computation.23 | async-start | bytes 4718592 | tf_op jit(solution)/shard_map/reduce_scatter | solution.py:121
  742.6 273.4 %reduce-scatter.23.cloned.1.call-start = ((), (), s32[]{:S(2)}) async-start(), calls=%async_computation.22 | async-start | bytes 4718592 | tf_op jit(solution)/shard_map/reduce_scatter | solution.py:121
  755.8 297.1 %reduce-scatter.17.cloned.1.call-start = ((), (), s32[]{:S(2)}) async-start(), calls=%async_computation.19 | async-start | bytes 2359296 | tf_op jit(solution)/shard_map/reduce_scatter | solution.py:121
  808.4 381.6 %reduce-scatter.31.cloned.1.call-start = ((), (), s32[]{:S(2)}) async-start(), calls=%async_computation.27 | async-start | bytes 1081344
  814.4 16.6 %collective-permute-start.30 = (bf16[192,2048]{1,0:T(8,128)(2,1)S(1)}, bf16[192,2048]{1,0:T(8,128)(2,1)S(1)}, u32[]{:S(2)}, u32[]{:S(2)}) collective-permute-start(bf16[192,2048]{1,0:T(8,128)(2,1)S(1)} %get-tuple-element.74), channel_id=1, source_target_pairs={{0,1},{1,0},{2,3},{3,2},{4,5},{5,4},{6,7},{7,6},{8,9},{9,8},{10,11... | collective-permute-start | bytes 2359304 | tf_op jit(solution)/shard_map/ppermute | solution.py:82
  817.4 19.6 %collective-permute-start.28 = (bf16[192,2048]{1,0:T(8,128)(2,1)S(1)}, bf16[192,2048]{1,0:T(8,128)(2,1)S(1)}, u32[]{:S(2)}, u32[]{:S(2)}) collective-permute-start(bf16[192,2048]{1,0:T(8,128)(2,1)S(1)} %get-tuple-element.73), channel_id=1, source_target_pairs={{0,2},{1,3},{2,0},{3,1},{4,6},{5,7},{6,4},{7,5},{8,10},{9,11},{10,... | collective-permute-start | bytes 2359304 | tf_op jit(solution)/shard_map/ppermute | solution.py:82
  831.3 39.4 %collective-permute-start.31 = (bf16[384,2048]{1,0:T(8,128)(2,1)S(1)}, bf16[384,2048]{1,0:T(8,128)(2,1)S(1)}, u32[]{:S(2)}, u32[]{:S(2)}) collective-permute-start(bf16[384,2048]{1,0:T(8,128)(2,1)S(1)} %pad_maximum_fusion.11), channel_id=1, source_target_pairs={{0,2},{1,3},{2,0},{3,1},{4,6},{5,7},{6,4},{7,5},{8,10},{9,11},{10,... | collective-permute-start | bytes 4718600 | tf_op jit(solution)/shard_map/ppermute | solution.py:82
  837.4 37.3 %collective-permute-start.29 = (bf16[384,2048]{1,0:T(8,128)(2,1)S(1)}, bf16[384,2048]{1,0:T(8,128)(2,1)S(1)}, u32[]{:S(2)}, u32[]{:S(2)}) collective-permute-start(bf16[384,2048]{1,0:T(8,128)(2,1)S(1)} %pad_maximum_fusion.10), channel_id=1, source_target_pairs={{0,1},{1,0},{2,3},{3,2},{4,5},{5,4},{6,7},{7,6},{8,9},{9,8},{10,11... | collective-permute-start | bytes 4718600 | tf_op jit(solution)/shard_map/ppermute | solution.py:82
  838.8 51.6 %collective-permute-start.14 = (bf16[192,2048]{1,0:T(8,128)(2,1)}, bf16[192,2048]{1,0:T(8,128)(2,1)}, u32[]{:S(2)}, u32[]{:S(2)}) collective-permute-start(bf16[192,2048]{1,0:T(8,128)(2,1)} %get-tuple-element.78), channel_id=1, source_target_pairs={{0,1},{1,0},{2,3},{3,2},{4,5},{5,4},{6,7},{7,6},{8,9},{9,8},{10,11... | collective-permute-start | bytes 2359304 | tf_op jit(solution)/shard_map/ppermute | solution.py:82
  840.8 52.7 %collective-permute-start.12 = (bf16[192,2048]{1,0:T(8,128)(2,1)}, bf16[192,2048]{1,0:T(8,128)(2,1)}, u32[]{:S(2)}, u32[]{:S(2)}) collective-permute-start(bf16[192,2048]{1,0:T(8,128)(2,1)} %get-tuple-element.77), channel_id=1, source_target_pairs={{0,2},{1,3},{2,0},{3,1},{4,6},{5,7},{6,4},{7,5},{8,10},{9,11},{10,... | collective-permute-start | bytes 2359304 | tf_op jit(solution)/shard_map/ppermute | solution.py:82
  845.1 29.7 %copy-start.10 = (bf16[384,2048]{1,0:T(8,128)(2,1)S(1)}, bf16[384,2048]{1,0:T(8,128)(2,1)}, u32[]{:S(2)}) copy-start(bf16[384,2048]{1,0:T(8,128)(2,1)} %param.13) | copy-start | bytes 4718596
  845.1 29.7 %copy-start.100 = (f32[2048,1]{0,1:T(1,128)S(1)}, f32[2048,1]{0,1:T(1,128)}, u32[]{:S(2)}) copy-start(f32[2048,1]{0,1:T(1,128)} %copy-done.99) | copy-start | bytes 24580
  845.1 29.7 %copy-start.105 = (f32[384]{0:T(512)S(1)}, f32[384]{0:T(512)}, u32[]{:S(2)}) copy-start(f32[384]{0:T(512)} %copy-done.104) | copy-start | bytes 4612
  850.9 30.9 %copy-start.63 = (bf16[1536,128]{0,1:T(8,128)(2,1)S(1)}, bf16[1536,128]{0,1:T(8,128)(2,1)}, u32[]{:S(2)}) copy-start(bf16[1536,128]{0,1:T(8,128)(2,1)} %copy-done.62) | copy-start | bytes 1179652
  881.6 347.3 %reduce-scatter.15.cloned.1.call-start = ((), (), s32[]{:S(2)}) async-start(), calls=%async_computation.18 | async-start | bytes 3538944 | tf_op jit(solution)/shard_map/reduce_scatter | solution.py:121
  892.5 25.8 %collective-permute-start.15 = (bf16[384,2048]{1,0:T(8,128)(2,1)S(1)}, bf16[384,2048]{1,0:T(8,128)(2,1)S(1)}, u32[]{:S(2)}, u32[]{:S(2)}) collective-permute-start(bf16[384,2048]{1,0:T(8,128)(2,1)S(1)} %pad_maximum_fusion.7), channel_id=1, source_target_pairs={{0,2},{1,3},{2,0},{3,1},{4,6},{5,7},{6,4},{7,5},{8,10},{9,11},{10,... | collective-permute-start | bytes 4718600 | tf_op jit(solution)/shard_map/ppermute | solution.py:82
  895.4 26.0 %collective-permute-start.13 = (bf16[384,2048]{1,0:T(8,128)(2,1)S(1)}, bf16[384,2048]{1,0:T(8,128)(2,1)S(1)}, u32[]{:S(2)}, u32[]{:S(2)}) collective-permute-start(bf16[384,2048]{1,0:T(8,128)(2,1)S(1)} %pad_maximum_fusion.6), channel_id=1, source_target_pairs={{0,1},{1,0},{2,3},{3,2},{4,5},{5,4},{6,7},{7,6},{8,9},{9,8},{10,11... | collective-permute-start | bytes 4718600 | tf_op jit(solution)/shard_map/ppermute | solution.py:82
  (162 other events, 1070.3 us)
Sparse Core Ops, SparseCore 0:
  12.3 59.1 all-gather.9
  105.9 26.7 all-gather.23
  134.3 46.2 all-gather.17
  182.1 45.6 all-gather.19
  229.8 46.6 all-gather.21
  277.9 45.0 all-gather.11
  324.6 45.6 all-gather.13
  371.9 46.6 all-gather.15
  678.3 34.1 reduce-scatter.12
  714.6 48.2 reduce-scatter.28
  765.2 48.3 reduce-scatter.26
  815.7 48.3 reduce-scatter.20
  866.5 48.3 reduce-scatter.18
  917.0 48.3 reduce-scatter.24
  967.6 48.3 reduce-scatter.22
  1018.2 34.6 reduce-scatter.16
  1054.9 134.9 reduce-scatter.30
  1192.1 36.6 reduce-scatter.14
